TPU v7x, 32 devices: a whole 2x2x4 slice. The times are simulated.
32 devices in a mesh: grp: 2 (over core), gx: 4 (over z), gy: 4 (over y, x).
Axes of the slice: x: 2, y: 2, z: 4, core: 2. Of those that a mesh axis runs over, the one named last changes fastest.
Arguments:
- gas_velocity: float32 [3, 64, 128, 384], P(None, 'gx', ('grp', 'gy')), may hold values from -6 to 6
- parcel_z: float32 [3072, 256], P(('grp', 'gx', 'gy')), may hold values from 0 to 383
- parcel_velocity: float32 [3072, 3, 256], P(('grp', 'gx', 'gy')), may hold values from -6 to 6
- parcel_rate: float32 [3072, 256], P(('grp', 'gx', 'gy')), may hold values from 0.05 to 5
- parcel_mass: float32 [3072, 256], P(('grp', 'gx', 'gy')), may hold values from 0.2 to 2
- parcel_column: int32 [3072], P(('grp', 'gx', 'gy')), may hold values from 0 to 8191, as said below
Outputs:
- gas_out: float32 [3, 64, 128, 384], P(None, 'gx', ('grp', 'gy'))
- parcel_out: float32 [6144, 3, 256], P(('grp', 'gx', 'gy'))
Inputs may be any that keep to these rules, and one draw needn't show every extreme that they name: `parcel_column`: each block's column lies in its own device's cells or in those of one of its four face neighbours along the first and second dimensions (cycles of 4 and 8 slabs). One device sends at most 24 blocks to one neighbour; in every draw some device keeps all its blocks and receives 24 blocks from each of its four neighbours.
All inputs are finite; a program needn't handle non-finite values.
Results may differ from a plain program's by a relative error of at most 0.0003.
Values sent between devices are 32-bit elements; how exact they have to be, the bound alone decides.
No kernel may reach another device: no remote copies, remote signals or barrier semaphores. Data moves between devices by JAX's collectives and lax.ppermute only.
A program may use at most 64 MiB of HBM per device.

v0:
```python
import math

import jax
import jax.numpy as jnp
from jax import lax
from jax.sharding import PartitionSpec as P

ITERS = 2


NU = 0.1


def with_halo(block, sides, width):
    for axis, dim in sides:
        count = lax.axis_size(axis)
        forward = [(i, i + 1) for i in range(count - 1)]
        forward.append((count - 1, 0))
        backward = [(target, source) for source, target in forward]
        low = lax.ppermute(
            lax.slice_in_dim(block, block.shape[dim] - width, None, axis=dim), axis, forward
        )
        high = lax.ppermute(lax.slice_in_dim(block, 0, width, axis=dim), axis, backward)
        block = jnp.concatenate([low, block, high], axis=dim)
    return block


def passed_along(value, axis, steps):
    count = lax.axis_size(axis)
    pairs = [(source, (source + steps) % count) for source in range(count)]
    return lax.ppermute(value, axis, pairs)


def diffuse_once(extended):
    center = extended[:, 1:-1, 1:-1]
    beside = (
        extended[:, 2:, 1:-1]
        + extended[:, :-2, 1:-1]
        + extended[:, 1:-1, 2:]
        + extended[:, 1:-1, :-2]
    )
    zeros_plane = jnp.zeros_like(center[..., :1])
    z_above = jnp.concatenate([center[..., 1:], zeros_plane], -1)
    z_below = jnp.concatenate([zeros_plane, center[..., :-1]], -1)
    return center + NU * (beside + z_above + z_below - 6.0 * center)


def heading(column, x_index, y_index, x_count, y_count, cells_x, cells_y, rows_total):
    target_x = column // rows_total // cells_x
    target_y = column % rows_total // cells_y
    return jnp.where(
        target_x == (x_index + 1) % x_count,
        1,
        jnp.where(
            target_x == (x_index - 1) % x_count,
            2,
            jnp.where(
                target_y == (y_index + 1) % y_count,
                3,
                jnp.where(target_y == (y_index - 1) % y_count, 4, 0),
            ),
        ),
    ).astype(jnp.int32)


def pack(state, direction, capacity):
    slots = state.shape[0]
    flat = state.reshape(slots, -1)
    staying = state * (direction == 0).astype(jnp.float32)[:, None, None]
    chosen = jnp.stack([(direction == code).astype(jnp.int32) for code in range(1, 5)])
    position = jnp.cumsum(chosen, 1) - 1
    select = (
        (chosen[:, None, :] == 1)
        & (position[:, None, :] == jnp.arange(capacity, dtype=jnp.int32)[None, :, None])
    ).astype(jnp.float32)
    outbox = jnp.einsum("cms,sk->cmk", select, flat, precision=lax.Precision.HIGHEST)
    return (staying, outbox.reshape(4, capacity, state.shape[1], state.shape[2]))


def couple_group(inputs):
    rows_g, positions, velocity, rates, masses = inputs
    depth = rows_g.shape[-1]
    cell_low = jnp.minimum(jnp.floor(positions).astype(jnp.int32), depth - 2)
    fraction = positions - cell_low.astype(jnp.float32)
    levels = jnp.arange(depth, dtype=jnp.int32)[None, None, :]
    hat = (1.0 - fraction)[..., None] * (levels == cell_low[..., None]).astype(
        jnp.float32
    ) + fraction[..., None] * (levels == (cell_low + 1)[..., None]).astype(jnp.float32)
    gas_at = jnp.einsum("cbz,bpz->cbp", rows_g, hat, precision=lax.Precision.HIGHEST)
    relax = rates / (1.0 + rates)
    updated = velocity + relax[None] * (gas_at - velocity)
    momentum = masses[None] * (velocity - updated)
    source_rows = jnp.einsum("cbp,bpz->cbz", momentum, hat, precision=lax.Precision.HIGHEST)
    return (updated, source_rows)


def body(gas_velocity, parcel_z, parcel_velocity, parcel_rate, parcel_mass, parcel_column):
    field = gas_velocity
    extended = with_halo(field, (("gx", 1), (("grp", "gy"), 2)), ITERS)
    for substep in range(ITERS):
        extended = diffuse_once(extended)
    field = extended
    cells_x = field.shape[1]
    cells_y = field.shape[2]
    depth = field.shape[3]
    slots = parcel_z.shape[0]
    width = parcel_z.shape[1]
    x_count = lax.axis_size("gx")
    y_count = lax.axis_size(("grp", "gy"))
    x_index = lax.axis_index("gx")
    y_index = lax.axis_index(("grp", "gy"))
    rows_total = cells_y * y_count
    column_f = parcel_column.astype(jnp.float32)
    state = jnp.concatenate(
        [
            parcel_z[:, None, :],
            parcel_velocity,
            parcel_rate[:, None, :],
            parcel_mass[:, None, :],
            jnp.broadcast_to(column_f[:, None, None], (slots, 1, width)),
        ],
        1,
    )
    direction = heading(
        parcel_column, x_index, y_index, x_count, y_count, cells_x, cells_y, rows_total
    )
    staying, outbox = pack(state, direction, slots // 4)
    received = []
    for code, offset in ((0, 1), (1, -1)):
        received.append(passed_along(outbox[code], "gx", offset))
    for code, offset in ((2, 1), (3, -1)):
        received.append(passed_along(outbox[code], ("grp", "gy"), offset))
    slotted = jnp.concatenate([staying] + received, 0)
    total_slots = slotted.shape[0]
    group_size = math.gcd(total_slots, 16)
    groups = total_slots // group_size
    column = slotted[:, 6, 0].astype(jnp.int32)
    local_column = column // rows_total % cells_x * cells_y + column % rows_total % cells_y
    lines = field.reshape(3, cells_x * cells_y, depth)
    rows = lines[:, local_column]
    rows_grouped = jnp.moveaxis(rows.reshape(3, groups, group_size, depth), 1, 0)
    positions = slotted[:, 0].reshape(groups, group_size, width)
    velocity = jnp.moveaxis(slotted[:, 1:4].reshape(groups, group_size, 3, width), 2, 1)
    rates = slotted[:, 4].reshape(groups, group_size, width)
    masses = slotted[:, 5].reshape(groups, group_size, width)
    updated, source_rows = lax.map(couple_group, (rows_grouped, positions, velocity, rates, masses))
    source_rows = jnp.moveaxis(source_rows, 1, 0).reshape(3, total_slots, depth)
    placement = (
        jnp.arange(cells_x * cells_y, dtype=jnp.int32)[:, None] == local_column[None, :]
    ).astype(jnp.float32)
    source = jnp.einsum("ls,csz->clz", placement, source_rows, precision=lax.Precision.HIGHEST)
    gas_out = (lines + source).reshape(3, cells_x, cells_y, depth)
    parcel_out = jnp.moveaxis(updated, 1, 2).reshape(total_slots, 3, width)
    return (gas_out, parcel_out)


def solution(mesh):
    placed = (
        P(None, "gx", ("grp", "gy"), None),
        P(("grp", "gx", "gy"), None),
        P(("grp", "gx", "gy"), None, None),
        P(("grp", "gx", "gy"), None),
        P(("grp", "gx", "gy"), None),
        P(("grp", "gx", "gy")),
    )
    return jax.shard_map(
        body,
        mesh=mesh,
        in_specs=placed,
        out_specs=(P(None, "gx", ("grp", "gy"), None), P(("grp", "gx", "gy"), None, None)),
        check_vma=False,
    )
```

profile of v0, /device:TPU:0, one launch (start us, length us, event | category | flops | bytes accessed | tf_op | source)
XLA Modules:
  0.0 247.7 jit_solution(8097270975370813334)
XLA Ops:
  2.4 5.1 %collective-permute-start.1 = (f32[3,2,16,384]{3,2,1,0:T(8,128)}, f32[3,2,16,384]{3,2,1,0:T(8,128)}, u32[]{:S(2)}, u32[]{:S(2)}) collective-permute-start(f32[3,2,16,384]{3,2,1,0:T(8,128)} %get-tuple-element.84), channel_id=1, source_target_pairs={{4,0},{8,4},{12,8},{0,12},{5,1},{9,5},{13,9},{1,13},{6,2},{10,6},{... | collective-permute-start | bytes 442376 | tf_op jit(solution)/shard_map/ppermute | solution.py:23
  15.5 3.8 %collective-permute-start.5 = (f32[24,7,256]{2,1,0:T(8,128)}, f32[24,7,256]{2,1,0:T(8,128)}, u32[]{:S(2)}, u32[]{:S(2)}) collective-permute-start(f32[24,7,256]{2,1,0:T(8,128)} %squeeze.28), channel_id=1, source_target_pairs={{0,12},{4,0},{8,4},{12,8},{1,13},{5,1},{9,5},{13,9},{2,14},{6,2},{... | collective-permute-start | bytes 516104 | tf_op jit(solution)/shard_map/ppermute | solution.py:31
  28.3 1.8 collective-permute-start.3
  36.9 3.8 %collective-permute-done.3 = f32[3,20,2,384]{3,1,2,0:T(8,128)S(1)} collective-permute-done((f32[3,20,2,384]{3,1,2,0:T(8,128)S(1)}, f32[3,20,2,384]{3,1,2,0:T(8,128)S(1)}, u32[]{:S(2)}, u32[]{:S(2)}) %collective-permute-start.3) | collective-permute-done | bytes 184352 | tf_op jit(solution)/shard_map/ppermute | solution.py:23
  41.9 2.8 %fusion.36 = f32[3,18,18,384]{3,1,2,0:T(8,128)S(1)} fusion(f32[3,20,2,384]{3,1,2,0:T(8,128)S(1)} %collective-permute-done.2, f32[3,2,16,384]{3,1,2,0:T(2,128)S(1)} %copy.50, f32[3,16,16,384]{3,1,2,0:T(8,128)S(1)} %copy.49, f32[3,2,16,384]{3,1,2,0:T(2,128)S(1)} %copy.48, f32[3,20,2,384]{3,1,2,0:T(8,128)S(1)} %collective-permute-done.3, ...), kind=kLoop, calls=%fused_computation.49 | loop fusion | flops 5598720 | bytes 10793376 | tf_op jit(solution)/shard_map/add | solution.py:45
  47.1 2.4 gather_fusion
  49.5 194.9 %while.12 = (s32[]{:T(128)}, f32[12,3,16,256]{3,1,2,0:T(4,128)S(1)}, f32[12,3,16,384]{3,1,2,0:T(4,128)}, f32[12,3,16,256]{3,1,2,0:T(4,128)}, f32[12,16,256]{2,1,...) while((s32[]{:T(128)}, ...), condition=%wide.region_2.3_spmd, body=%wide.region_1.2_spmd.sunk | while | flops 129073152 | bytes 837741 | solution.py:146
  51.0 8.2 %bitcast_dynamic-update-slice_fusion.5 = (f32[12,3,16,256]{3,1,2,0:T(4,128)S(1)}, f32[3,16,256]{2,0,1:T(4,128)S(1)}) fusion(f32[12,3,16,256]{3,1,2,0:T(4,128)S(1)} %get-tuple-element.166, s32[]{:T(128)S(6)} %copy.80, f32[12,3,16,384]{3,1,2,0:T(4,128)} %get-tuple-element.180, f32[16,256]{1,0:T(8,128)S(1)} %get-tuple-element.149, ...), kind=kOutput, calls=%fused_computation.24.clone.1 | convolution fusion | flops 64524288 | bytes 377856 | tf_op jit(solution)/shard_map/while/body/eval_jaxpr/cbz,bpz->cbp/dot_general | solution.py:89
  59.2 6.6 %fusion.74 = f32[12,3,16,384]{3,1,2,0:T(4,128)} fusion(f32[12,3,16,384]{3,1,2,0:T(4,128)} %get-tuple-element.167, s32[]{:T(128)S(6)} %copy.80, f32[16,256]{1,0:T(8,128)S(1)} %get-tuple-element.149, s32[16,256]{1,0:T(8,128)S(1)} %broadcast_add_fusion.3, f32[16,256]{1,0:T(8,128)S(1)} %get-tuple-element.151, s32[16,256]{1,0:T(8,128)S(1)} %get-tuple-element.150, ...), kind=kOutput, calls=%fused_computation.17.clone.1 | convolution fusion | flops 64512000 | bytes 295936 | tf_op jit(solution)/shard_map/while/body/eval_jaxpr/cbp,bpz->cbz/dot_general | solution.py:93
  67.2 8.2 %bitcast_dynamic-update-slice_fusion.5 = (f32[12,3,16,256]{3,1,2,0:T(4,128)S(1)}, f32[3,16,256]{2,0,1:T(4,128)S(1)}) fusion(f32[12,3,16,256]{3,1,2,0:T(4,128)S(1)} %get-tuple-element.166, s32[]{:T(128)S(6)} %copy.80, f32[12,3,16,384]{3,1,2,0:T(4,128)} %get-tuple-element.180, f32[16,256]{1,0:T(8,128)S(1)} %get-tuple-element.149, ...), kind=kOutput, calls=%fused_computation.24.clone.1 | convolution fusion | flops 64524288 | bytes 377856 | tf_op jit(solution)/shard_map/while/body/eval_jaxpr/cbz,bpz->cbp/dot_general | solution.py:89
  75.4 6.6 %fusion.74 = f32[12,3,16,384]{3,1,2,0:T(4,128)} fusion(f32[12,3,16,384]{3,1,2,0:T(4,128)} %get-tuple-element.167, s32[]{:T(128)S(6)} %copy.80, f32[16,256]{1,0:T(8,128)S(1)} %get-tuple-element.149, s32[16,256]{1,0:T(8,128)S(1)} %broadcast_add_fusion.3, f32[16,256]{1,0:T(8,128)S(1)} %get-tuple-element.151, s32[16,256]{1,0:T(8,128)S(1)} %get-tuple-element.150, ...), kind=kOutput, calls=%fused_computation.17.clone.1 | convolution fusion | flops 64512000 | bytes 295936 | tf_op jit(solution)/shard_map/while/body/eval_jaxpr/cbp,bpz->cbz/dot_general | solution.py:93
  83.5 8.2 %bitcast_dynamic-update-slice_fusion.5 = (f32[12,3,16,256]{3,1,2,0:T(4,128)S(1)}, f32[3,16,256]{2,0,1:T(4,128)S(1)}) fusion(f32[12,3,16,256]{3,1,2,0:T(4,128)S(1)} %get-tuple-element.166, s32[]{:T(128)S(6)} %copy.80, f32[12,3,16,384]{3,1,2,0:T(4,128)} %get-tuple-element.180, f32[16,256]{1,0:T(8,128)S(1)} %get-tuple-element.149, ...), kind=kOutput, calls=%fused_computation.24.clone.1 | convolution fusion | flops 64524288 | bytes 377856 | tf_op jit(solution)/shard_map/while/body/eval_jaxpr/cbz,bpz->cbp/dot_general | solution.py:89
  91.7 6.6 %fusion.74 = f32[12,3,16,384]{3,1,2,0:T(4,128)} fusion(f32[12,3,16,384]{3,1,2,0:T(4,128)} %get-tuple-element.167, s32[]{:T(128)S(6)} %copy.80, f32[16,256]{1,0:T(8,128)S(1)} %get-tuple-element.149, s32[16,256]{1,0:T(8,128)S(1)} %broadcast_add_fusion.3, f32[16,256]{1,0:T(8,128)S(1)} %get-tuple-element.151, s32[16,256]{1,0:T(8,128)S(1)} %get-tuple-element.150, ...), kind=kOutput, calls=%fused_computation.17.clone.1 | convolution fusion | flops 64512000 | bytes 295936 | tf_op jit(solution)/shard_map/while/body/eval_jaxpr/cbp,bpz->cbz/dot_general | solution.py:93
  99.7 8.2 %bitcast_dynamic-update-slice_fusion.5 = (f32[12,3,16,256]{3,1,2,0:T(4,128)S(1)}, f32[3,16,256]{2,0,1:T(4,128)S(1)}) fusion(f32[12,3,16,256]{3,1,2,0:T(4,128)S(1)} %get-tuple-element.166, s32[]{:T(128)S(6)} %copy.80, f32[12,3,16,384]{3,1,2,0:T(4,128)} %get-tuple-element.180, f32[16,256]{1,0:T(8,128)S(1)} %get-tuple-element.149, ...), kind=kOutput, calls=%fused_computation.24.clone.1 | convolution fusion | flops 64524288 | bytes 377856 | tf_op jit(solution)/shard_map/while/body/eval_jaxpr/cbz,bpz->cbp/dot_general | solution.py:89
  107.9 6.6 %fusion.74 = f32[12,3,16,384]{3,1,2,0:T(4,128)} fusion(f32[12,3,16,384]{3,1,2,0:T(4,128)} %get-tuple-element.167, s32[]{:T(128)S(6)} %copy.80, f32[16,256]{1,0:T(8,128)S(1)} %get-tuple-element.149, s32[16,256]{1,0:T(8,128)S(1)} %broadcast_add_fusion.3, f32[16,256]{1,0:T(8,128)S(1)} %get-tuple-element.151, s32[16,256]{1,0:T(8,128)S(1)} %get-tuple-element.150, ...), kind=kOutput, calls=%fused_computation.17.clone.1 | convolution fusion | flops 64512000 | bytes 295936 | tf_op jit(solution)/shard_map/while/body/eval_jaxpr/cbp,bpz->cbz/dot_general | solution.py:93
  116.0 8.2 %bitcast_dynamic-update-slice_fusion.5 = (f32[12,3,16,256]{3,1,2,0:T(4,128)S(1)}, f32[3,16,256]{2,0,1:T(4,128)S(1)}) fusion(f32[12,3,16,256]{3,1,2,0:T(4,128)S(1)} %get-tuple-element.166, s32[]{:T(128)S(6)} %copy.80, f32[12,3,16,384]{3,1,2,0:T(4,128)} %get-tuple-element.180, f32[16,256]{1,0:T(8,128)S(1)} %get-tuple-element.149, ...), kind=kOutput, calls=%fused_computation.24.clone.1 | convolution fusion | flops 64524288 | bytes 377856 | tf_op jit(solution)/shard_map/while/body/eval_jaxpr/cbz,bpz->cbp/dot_general | solution.py:89
  124.1 6.6 %fusion.74 = f32[12,3,16,384]{3,1,2,0:T(4,128)} fusion(f32[12,3,16,384]{3,1,2,0:T(4,128)} %get-tuple-element.167, s32[]{:T(128)S(6)} %copy.80, f32[16,256]{1,0:T(8,128)S(1)} %get-tuple-element.149, s32[16,256]{1,0:T(8,128)S(1)} %broadcast_add_fusion.3, f32[16,256]{1,0:T(8,128)S(1)} %get-tuple-element.151, s32[16,256]{1,0:T(8,128)S(1)} %get-tuple-element.150, ...), kind=kOutput, calls=%fused_computation.17.clone.1 | convolution fusion | flops 64512000 | bytes 295936 | tf_op jit(solution)/shard_map/while/body/eval_jaxpr/cbp,bpz->cbz/dot_general | solution.py:93
  132.2 8.2 %bitcast_dynamic-update-slice_fusion.5 = (f32[12,3,16,256]{3,1,2,0:T(4,128)S(1)}, f32[3,16,256]{2,0,1:T(4,128)S(1)}) fusion(f32[12,3,16,256]{3,1,2,0:T(4,128)S(1)} %get-tuple-element.166, s32[]{:T(128)S(6)} %copy.80, f32[12,3,16,384]{3,1,2,0:T(4,128)} %get-tuple-element.180, f32[16,256]{1,0:T(8,128)S(1)} %get-tuple-element.149, ...), kind=kOutput, calls=%fused_computation.24.clone.1 | convolution fusion | flops 64524288 | bytes 377856 | tf_op jit(solution)/shard_map/while/body/eval_jaxpr/cbz,bpz->cbp/dot_general | solution.py:89
  140.4 6.6 %fusion.74 = f32[12,3,16,384]{3,1,2,0:T(4,128)} fusion(f32[12,3,16,384]{3,1,2,0:T(4,128)} %get-tuple-element.167, s32[]{:T(128)S(6)} %copy.80, f32[16,256]{1,0:T(8,128)S(1)} %get-tuple-element.149, s32[16,256]{1,0:T(8,128)S(1)} %broadcast_add_fusion.3, f32[16,256]{1,0:T(8,128)S(1)} %get-tuple-element.151, s32[16,256]{1,0:T(8,128)S(1)} %get-tuple-element.150, ...), kind=kOutput, calls=%fused_computation.17.clone.1 | convolution fusion | flops 64512000 | bytes 295936 | tf_op jit(solution)/shard_map/while/body/eval_jaxpr/cbp,bpz->cbz/dot_general | solution.py:93
  148.4 8.2 %bitcast_dynamic-update-slice_fusion.5 = (f32[12,3,16,256]{3,1,2,0:T(4,128)S(1)}, f32[3,16,256]{2,0,1:T(4,128)S(1)}) fusion(f32[12,3,16,256]{3,1,2,0:T(4,128)S(1)} %get-tuple-element.166, s32[]{:T(128)S(6)} %copy.80, f32[12,3,16,384]{3,1,2,0:T(4,128)} %get-tuple-element.180, f32[16,256]{1,0:T(8,128)S(1)} %get-tuple-element.149, ...), kind=kOutput, calls=%fused_computation.24.clone.1 | convolution fusion | flops 64524288 | bytes 377856 | tf_op jit(solution)/shard_map/while/body/eval_jaxpr/cbz,bpz->cbp/dot_general | solution.py:89
  156.6 6.6 %fusion.74 = f32[12,3,16,384]{3,1,2,0:T(4,128)} fusion(f32[12,3,16,384]{3,1,2,0:T(4,128)} %get-tuple-element.167, s32[]{:T(128)S(6)} %copy.80, f32[16,256]{1,0:T(8,128)S(1)} %get-tuple-element.149, s32[16,256]{1,0:T(8,128)S(1)} %broadcast_add_fusion.3, f32[16,256]{1,0:T(8,128)S(1)} %get-tuple-element.151, s32[16,256]{1,0:T(8,128)S(1)} %get-tuple-element.150, ...), kind=kOutput, calls=%fused_computation.17.clone.1 | convolution fusion | flops 64512000 | bytes 295936 | tf_op jit(solution)/shard_map/while/body/eval_jaxpr/cbp,bpz->cbz/dot_general | solution.py:93
  164.7 8.2 %bitcast_dynamic-update-slice_fusion.5 = (f32[12,3,16,256]{3,1,2,0:T(4,128)S(1)}, f32[3,16,256]{2,0,1:T(4,128)S(1)}) fusion(f32[12,3,16,256]{3,1,2,0:T(4,128)S(1)} %get-tuple-element.166, s32[]{:T(128)S(6)} %copy.80, f32[12,3,16,384]{3,1,2,0:T(4,128)} %get-tuple-element.180, f32[16,256]{1,0:T(8,128)S(1)} %get-tuple-element.149, ...), kind=kOutput, calls=%fused_computation.24.clone.1 | convolution fusion | flops 64524288 | bytes 377856 | tf_op jit(solution)/shard_map/while/body/eval_jaxpr/cbz,bpz->cbp/dot_general | solution.py:89
  172.9 6.6 %fusion.74 = f32[12,3,16,384]{3,1,2,0:T(4,128)} fusion(f32[12,3,16,384]{3,1,2,0:T(4,128)} %get-tuple-element.167, s32[]{:T(128)S(6)} %copy.80, f32[16,256]{1,0:T(8,128)S(1)} %get-tuple-element.149, s32[16,256]{1,0:T(8,128)S(1)} %broadcast_add_fusion.3, f32[16,256]{1,0:T(8,128)S(1)} %get-tuple-element.151, s32[16,256]{1,0:T(8,128)S(1)} %get-tuple-element.150, ...), kind=kOutput, calls=%fused_computation.17.clone.1 | convolution fusion | flops 64512000 | bytes 295936 | tf_op jit(solution)/shard_map/while/body/eval_jaxpr/cbp,bpz->cbz/dot_general | solution.py:93
  180.9 8.2 %bitcast_dynamic-update-slice_fusion.5 = (f32[12,3,16,256]{3,1,2,0:T(4,128)S(1)}, f32[3,16,256]{2,0,1:T(4,128)S(1)}) fusion(f32[12,3,16,256]{3,1,2,0:T(4,128)S(1)} %get-tuple-element.166, s32[]{:T(128)S(6)} %copy.80, f32[12,3,16,384]{3,1,2,0:T(4,128)} %get-tuple-element.180, f32[16,256]{1,0:T(8,128)S(1)} %get-tuple-element.149, ...), kind=kOutput, calls=%fused_computation.24.clone.1 | convolution fusion | flops 64524288 | bytes 377856 | tf_op jit(solution)/shard_map/while/body/eval_jaxpr/cbz,bpz->cbp/dot_general | solution.py:89
  189.1 6.6 %fusion.74 = f32[12,3,16,384]{3,1,2,0:T(4,128)} fusion(f32[12,3,16,384]{3,1,2,0:T(4,128)} %get-tuple-element.167, s32[]{:T(128)S(6)} %copy.80, f32[16,256]{1,0:T(8,128)S(1)} %get-tuple-element.149, s32[16,256]{1,0:T(8,128)S(1)} %broadcast_add_fusion.3, f32[16,256]{1,0:T(8,128)S(1)} %get-tuple-element.151, s32[16,256]{1,0:T(8,128)S(1)} %get-tuple-element.150, ...), kind=kOutput, calls=%fused_computation.17.clone.1 | convolution fusion | flops 64512000 | bytes 295936 | tf_op jit(solution)/shard_map/while/body/eval_jaxpr/cbp,bpz->cbz/dot_general | solution.py:93
  197.2 8.2 %bitcast_dynamic-update-slice_fusion.5 = (f32[12,3,16,256]{3,1,2,0:T(4,128)S(1)}, f32[3,16,256]{2,0,1:T(4,128)S(1)}) fusion(f32[12,3,16,256]{3,1,2,0:T(4,128)S(1)} %get-tuple-element.166, s32[]{:T(128)S(6)} %copy.80, f32[12,3,16,384]{3,1,2,0:T(4,128)} %get-tuple-element.180, f32[16,256]{1,0:T(8,128)S(1)} %get-tuple-element.149, ...), kind=kOutput, calls=%fused_computation.24.clone.1 | convolution fusion | flops 64524288 | bytes 377856 | tf_op jit(solution)/shard_map/while/body/eval_jaxpr/cbz,bpz->cbp/dot_general | solution.py:89
  205.4 6.6 %fusion.74 = f32[12,3,16,384]{3,1,2,0:T(4,128)} fusion(f32[12,3,16,384]{3,1,2,0:T(4,128)} %get-tuple-element.167, s32[]{:T(128)S(6)} %copy.80, f32[16,256]{1,0:T(8,128)S(1)} %get-tuple-element.149, s32[16,256]{1,0:T(8,128)S(1)} %broadcast_add_fusion.3, f32[16,256]{1,0:T(8,128)S(1)} %get-tuple-element.151, s32[16,256]{1,0:T(8,128)S(1)} %get-tuple-element.150, ...), kind=kOutput, calls=%fused_computation.17.clone.1 | convolution fusion | flops 64512000 | bytes 295936 | tf_op jit(solution)/shard_map/while/body/eval_jaxpr/cbp,bpz->cbz/dot_general | solution.py:93
  213.4 8.2 %bitcast_dynamic-update-slice_fusion.5 = (f32[12,3,16,256]{3,1,2,0:T(4,128)S(1)}, f32[3,16,256]{2,0,1:T(4,128)S(1)}) fusion(f32[12,3,16,256]{3,1,2,0:T(4,128)S(1)} %get-tuple-element.166, s32[]{:T(128)S(6)} %copy.80, f32[12,3,16,384]{3,1,2,0:T(4,128)} %get-tuple-element.180, f32[16,256]{1,0:T(8,128)S(1)} %get-tuple-element.149, ...), kind=kOutput, calls=%fused_computation.24.clone.1 | convolution fusion | flops 64524288 | bytes 377856 | tf_op jit(solution)/shard_map/while/body/eval_jaxpr/cbz,bpz->cbp/dot_general | solution.py:89
  221.6 6.6 %fusion.74 = f32[12,3,16,384]{3,1,2,0:T(4,128)} fusion(f32[12,3,16,384]{3,1,2,0:T(4,128)} %get-tuple-element.167, s32[]{:T(128)S(6)} %copy.80, f32[16,256]{1,0:T(8,128)S(1)} %get-tuple-element.149, s32[16,256]{1,0:T(8,128)S(1)} %broadcast_add_fusion.3, f32[16,256]{1,0:T(8,128)S(1)} %get-tuple-element.151, s32[16,256]{1,0:T(8,128)S(1)} %get-tuple-element.150, ...), kind=kOutput, calls=%fused_computation.17.clone.1 | convolution fusion | flops 64512000 | bytes 295936 | tf_op jit(solution)/shard_map/while/body/eval_jaxpr/cbp,bpz->cbz/dot_general | solution.py:93
  229.7 8.2 %bitcast_dynamic-update-slice_fusion.5 = (f32[12,3,16,256]{3,1,2,0:T(4,128)S(1)}, f32[3,16,256]{2,0,1:T(4,128)S(1)}) fusion(f32[12,3,16,256]{3,1,2,0:T(4,128)S(1)} %get-tuple-element.166, s32[]{:T(128)S(6)} %copy.80, f32[12,3,16,384]{3,1,2,0:T(4,128)} %get-tuple-element.180, f32[16,256]{1,0:T(8,128)S(1)} %get-tuple-element.149, ...), kind=kOutput, calls=%fused_computation.24.clone.1 | convolution fusion | flops 64524288 | bytes 377856 | tf_op jit(solution)/shard_map/while/body/eval_jaxpr/cbz,bpz->cbp/dot_general | solution.py:89
  237.8 6.6 %fusion.74 = f32[12,3,16,384]{3,1,2,0:T(4,128)} fusion(f32[12,3,16,384]{3,1,2,0:T(4,128)} %get-tuple-element.167, s32[]{:T(128)S(6)} %copy.80, f32[16,256]{1,0:T(8,128)S(1)} %get-tuple-element.149, s32[16,256]{1,0:T(8,128)S(1)} %broadcast_add_fusion.3, f32[16,256]{1,0:T(8,128)S(1)} %get-tuple-element.151, s32[16,256]{1,0:T(8,128)S(1)} %get-tuple-element.150, ...), kind=kOutput, calls=%fused_computation.17.clone.1 | convolution fusion | flops 64512000 | bytes 295936 | tf_op jit(solution)/shard_map/while/body/eval_jaxpr/cbp,bpz->cbz/dot_general | solution.py:93
  245.9 1.9 fusion.38
  (95 shorter events, 48.2 us)
Async XLA Ops:
  2.4 21.8 %collective-permute-start.1 = (f32[3,2,16,384]{3,2,1,0:T(8,128)}, f32[3,2,16,384]{3,2,1,0:T(8,128)}, u32[]{:S(2)}, u32[]{:S(2)}) collective-permute-start(f32[3,2,16,384]{3,2,1,0:T(8,128)} %get-tuple-element.84), channel_id=1, source_target_pairs={{4,0},{8,4},{12,8},{0,12},{5,1},{9,5},{13,9},{1,13},{6,2},{10,6},{... | collective-permute-start | bytes 442376 | tf_op jit(solution)/shard_map/ppermute | solution.py:23
  7.4 18.8 %collective-permute-start = (f32[3,2,16,384]{3,2,1,0:T(8,128)}, f32[3,2,16,384]{3,2,1,0:T(8,128)}, u32[]{:S(2)}, u32[]{:S(2)}) collective-permute-start(f32[3,2,16,384]{3,2,1,0:T(8,128)} %get-tuple-element.83), channel_id=1, source_target_pairs={{0,4},{4,8},{8,12},{12,0},{1,5},{5,9},{9,13},{13,1},{2,6},{6,10},{... | collective-permute-start | bytes 442376 | tf_op jit(solution)/shard_map/ppermute | solution.py:20
  14.8 13.5 %collective-permute-start.4 = (f32[24,7,256]{2,1,0:T(8,128)}, f32[24,7,256]{2,1,0:T(8,128)}, u32[]{:S(2)}, u32[]{:S(2)}) collective-permute-start(f32[24,7,256]{2,1,0:T(8,128)} %squeeze.27), channel_id=1, source_target_pairs={{0,4},{4,8},{8,12},{12,0},{1,5},{5,9},{9,13},{13,1},{2,6},{6,10},{... | collective-permute-start | bytes 516104 | tf_op jit(solution)/shard_map/ppermute | solution.py:31
  15.5 15.5 %collective-permute-start.5 = (f32[24,7,256]{2,1,0:T(8,128)}, f32[24,7,256]{2,1,0:T(8,128)}, u32[]{:S(2)}, u32[]{:S(2)}) collective-permute-start(f32[24,7,256]{2,1,0:T(8,128)} %squeeze.28), channel_id=1, source_target_pairs={{0,12},{4,0},{8,4},{12,8},{1,13},{5,1},{9,5},{13,9},{2,14},{6,2},{... | collective-permute-start | bytes 516104 | tf_op jit(solution)/shard_map/ppermute | solution.py:31
  20.1 11.9 %collective-permute-start.6 = (f32[24,7,256]{2,1,0:T(8,128)}, f32[24,7,256]{2,1,0:T(8,128)}, u32[]{:S(2)}, u32[]{:S(2)}) collective-permute-start(f32[24,7,256]{2,1,0:T(8,128)} %squeeze.29), channel_id=1, source_target_pairs={{0,1},{1,2},{2,3},{3,16},{16,17},{17,18},{18,19},{19,0},{4,5},{5,6... | collective-permute-start | bytes 516104 | tf_op jit(solution)/shard_map/ppermute | solution.py:31
  24.1 8.9 %collective-permute-start.7 = (f32[24,7,256]{2,1,0:T(8,128)}, f32[24,7,256]{2,1,0:T(8,128)S(1)}, u32[]{:S(2)}, u32[]{:S(2)}) collective-permute-start(f32[24,7,256]{2,1,0:T(8,128)} %squeeze.30), channel_id=1, source_target_pairs={{0,19},{1,0},{2,1},{3,2},{16,3},{17,16},{18,17},{19,18},{4,23},{5,... | collective-permute-start | bytes 516104 | tf_op jit(solution)/shard_map/ppermute | solution.py:31
  27.3 9.6 %collective-permute-start.2 = (f32[3,20,2,384]{3,1,2,0:T(8,128)S(1)}, f32[3,20,2,384]{3,1,2,0:T(8,128)S(1)}, u32[]{:S(2)}, u32[]{:S(2)}) collective-permute-start(f32[3,20,2,384]{3,1,2,0:T(8,128)S(1)} %get-tuple-element.79), channel_id=1, source_target_pairs={{0,1},{1,2},{2,3},{3,16},{16,17},{17,18},{18,19},{19,0},{4,5},{5,6... | collective-permute-start | bytes 552968 | tf_op jit(solution)/shard_map/ppermute | solution.py:20
  28.3 12.5 %collective-permute-start.3 = (f32[3,20,2,384]{3,1,2,0:T(8,128)S(1)}, f32[3,20,2,384]{3,1,2,0:T(8,128)S(1)}, u32[]{:S(2)}, u32[]{:S(2)}) collective-permute-start(f32[3,20,2,384]{3,1,2,0:T(8,128)S(1)} %get-tuple-element.78), channel_id=1, source_target_pairs={{1,0},{2,1},{3,2},{16,3},{17,16},{18,17},{19,18},{0,19},{5,4},{6,5... | collective-permute-start | bytes 552968 | tf_op jit(solution)/shard_map/ppermute | solution.py:23
  244.4 1.5 copy-start
where the time goes:
time: 252 us; the launch traced here: 248 us
  matrix products  179 us (71%)
  local copies, waits for them, and re-layouts  24.3 us (10%)
  other arithmetic  23.6 us (9%)
  starting transfers between devices  14.3 us (6%)
  waiting for transfers between devices  5.32 us (2%)
    dot_general x12, matrix products, couple_group(): jnp.einsum('cbz,bpz->cbp', rows_g, hat, precision=lax.Precision.HIGHEST)  98.2 us
    dot_general x12, matrix products, couple_group(): jnp.einsum('cbp,bpz->cbz', momentum, hat, precision=lax.Precision.HIGHEST)  78.8 us
    mul x12, other arithmetic, couple_group(): updated = velocity + relax[None] * (gas_at - velocity)  9 us
    unnamed x10, local copies, waits for them, and re-layouts  8.84 us
    sub x12, other arithmetic, couple_group(): 1.0 - fraction  8.71 us
    ppermute x2, starting transfers between devices, with_halo(): lax.ppermute(lax.slice_in_dim(block, 0, width, axis=dim), axis, backward)  6.85 us
    ppermute x4, starting transfers between devices, passed_along(): return lax.ppermute(value, axis, pairs)  6.47 us
  transfers between devices with their start and end apart: 8, of which 2 were waited for; matrix products, arithmetic and copies ran while one was open for 8% of the time, Pallas kernels for 0%

commit v1 on v0

v1 whole, which is shorter than its diff:
```python
import functools

import jax
import jax.numpy as jnp
from jax import lax
from jax.experimental import pallas as pl
from jax.experimental.pallas import tpu as pltpu
from jax.sharding import PartitionSpec as P

ITERS = 2
NU = 0.1
LANES = 128
SUB = 8
Y_AXES = ("grp", "gy")

VMEM = pl.BlockSpec(memory_space=pltpu.VMEM)
SMEM = pl.BlockSpec(memory_space=pltpu.SMEM)
ANY = pl.BlockSpec(memory_space=pl.ANY)


def y_place():
    return lax.axis_index("grp") * lax.axis_size("gy") + lax.axis_index("gy")


def heading_of(column, dims):
    x_count, y_count, cells_x, cells_y = dims
    rows_total = cells_y * y_count
    x_index, y_index = lax.axis_index("gx"), y_place()
    target_x = column // rows_total // cells_x
    target_y = column % rows_total // cells_y
    return jnp.where(
        target_x == (x_index + 1) % x_count,
        1,
        jnp.where(
            target_x == (x_index + x_count - 1) % x_count,
            2,
            jnp.where(
                target_y == (y_index + 1) % y_count,
                3,
                jnp.where(target_y == (y_index + y_count - 1) % y_count, 4, 0),
            ),
        ),
    )


def local_of(column, dims):
    x_count, y_count, cells_x, cells_y = dims
    rows_total = cells_y * y_count
    return column // rows_total % cells_x * cells_y + column % rows_total % cells_y


def faces_kernel(gas, x_up, x_down, y_up, y_down, pp, pm, mp, mm):
    comps, cells_x, cells_y, depth = gas.shape
    x_up[...] = gas[:, cells_x - 2 :]
    x_down[...] = gas[:, :2]
    for c in range(comps):
        for near in range(2):
            for out, y in ((y_up, cells_y - 2 + near), (y_down, near)):
                out[c, near] = gas[c, :, y, :]
        last_x, last_y = cells_x - 1, cells_y - 1
        for out, x, y in (
            (pp, last_x, last_y),
            (pm, last_x, 0),
            (mp, 0, last_y),
            (mm, 0, 0),
        ):
            out[pl.ds(c, 1), :] = gas[c, x, pl.ds(y, 1), :]


def pack_kernel(dims, capacity, columns, z, v, rate, mass, *refs):
    boxes, box = refs[:4], refs[4]
    slots, width = z.shape
    fields = 6
    rows = fields * capacity + SUB
    box[...] = jnp.zeros_like(box)
    lane = lax.broadcasted_iota(jnp.int32, (1, LANES), 1)

    def one(s, counts):
        column = columns[s]
        head = heading_of(column, dims)
        place = jnp.int32(0)
        for code in range(1, 5):
            place = jnp.where(head == code, counts[code - 1], place)
        counts = tuple(
            counts[code - 1] + (head == code).astype(jnp.int32) for code in range(1, 5)
        )
        ok = (head > 0) & (place < capacity)
        base = jnp.where(ok, (head - 1) * rows, 4 * rows)
        place = jnp.where(ok, place, 0)
        at = base + place
        box[pl.ds(at, 1), :] = z[pl.ds(s, 1), :]
        for c in range(3):
            box[pl.ds(at + (1 + c) * capacity, 1), :] = v[c, pl.ds(s, 1), :]
        box[pl.ds(at + 4 * capacity, 1), :] = rate[pl.ds(s, 1), :]
        box[pl.ds(at + 5 * capacity, 1), :] = mass[pl.ds(s, 1), :]
        tail = base + fields * capacity
        tail = pl.multiple_of(tail, SUB)
        kept = box[pl.ds(tail, 1), pl.ds(0, LANES)]
        box[pl.ds(tail, 1), pl.ds(0, LANES)] = jnp.where(
            lane == place, column.astype(jnp.float32), kept
        )
        return counts

    lax.fori_loop(0, slots, one, (jnp.int32(0),) * 4)
    for code in range(4):
        boxes[code][...] = box[code * rows : (code + 1) * rows, :]


def up_down(value):
    depth = value.shape[-1]
    axis = value.ndim - 1
    level = lax.broadcasted_iota(jnp.int32, value.shape, axis)
    above = jnp.where(level == depth - 1, 0.0, pltpu.roll(value, depth - 1, axis))
    below = jnp.where(level == 0, 0.0, pltpu.roll(value, 1, axis))
    return above + below


def couple_kernel(
    dims,
    capacity,
    columns,
    gas,
    x_low,
    x_high,
    y_low,
    y_high,
    ll,
    lh,
    hl,
    hh,
    z,
    v,
    rate,
    mass,
    in0,
    in1,
    in2,
    in3,
    gas_out,
    parcel_out,
    ext,
    mid,
    lines,
    acc,
    rows_scr,
    weights,
    cells_scr,
    arrived,
    sems,
):
    x_count, y_count, cells_x, cells_y = dims
    comps, _, _, depth = gas.shape
    slots, width = z.shape
    chunks = depth // LANES
    tiles = width // LANES
    top = SUB
    pitch = lines.shape[0] // (cells_x * cells_y)
    acc_pitch = acc.shape[0] // (cells_x * cells_y)
    half = acc_pitch
    inboxes = (in0, in1, in2, in3)

    own = pltpu.make_async_copy(
        gas, ext.at[:, pl.ds(2, cells_x), pl.ds(top, cells_y), :], sems.at[0]
    )
    own.start()
    tails = []
    for code in range(4):
        tail = pltpu.make_async_copy(
            inboxes[code].at[pl.ds(6 * capacity, SUB), pl.ds(0, LANES)],
            arrived.at[pl.ds(code * SUB, SUB), :],
            sems.at[1 + code],
        )
        tail.start()
        tails.append(tail)
    acc[...] = jnp.zeros_like(acc)
    own.wait()

    ext[:, 0:2, top : top + cells_y, :] = x_low[...]
    ext[:, 2 + cells_x : 4 + cells_x, top : top + cells_y, :] = x_high[...]
    for c in range(comps):
        ext[c, 2 : 2 + cells_x, top - 1, :] = y_low[c, 1]
        ext[c, 2 : 2 + cells_x, top + cells_y, :] = y_high[c, 0]
        for corner, x, y in (
            (ll, 1, top - 1),
            (lh, 1, top + cells_y),
            (hl, 2 + cells_x, top - 1),
            (hh, 2 + cells_x, top + cells_y),
        ):
            ext[c, x, pl.ds(y, 1), :] = corner[pl.ds(c, 1), :]

    def first_plane(i, carry):
        x = 1 + i
        for c in range(comps):
            center = ext[c, x, pl.ds(top, cells_y), :]
            beside = (
                ext[c, x + 1, pl.ds(top, cells_y), :]
                + ext[c, x - 1, pl.ds(top, cells_y), :]
                + ext[c, x, pl.ds(top + 1, cells_y), :]
                + ext[c, x, pl.ds(top - 1, cells_y), :]
            )
            mid[c, i, pl.ds(top, cells_y), :] = center + NU * (
                beside + up_down(center) - 6.0 * center
            )
        return carry

    lax.fori_loop(0, cells_x + 2, first_plane, 0)

    x_row = lax.broadcasted_iota(jnp.int32, (cells_x, depth), 0)
    for c in range(comps):
        for face, near, far, inner, low_c, high_c, row in (
            (y_low, 1, 0, top, ll, hl, top - 1),
            (y_high, 0, 1, top + cells_y - 1, lh, hh, top + cells_y),
        ):
            center = face[c, near]
            left = jnp.where(
                x_row == 0, low_c[pl.ds(c, 1), :], pltpu.roll(center, 1, 0)
            )
            right = jnp.where(
                x_row == cells_x - 1,
                high_c[pl.ds(c, 1), :],
                pltpu.roll(center, cells_x - 1, 0),
            )
            inside = ext[c, 2 : 2 + cells_x, inner, :]
            beside = left + right + face[c, far] + inside
            mid[c, 1 : 1 + cells_x, row, :] = center + NU * (
                beside + up_down(center) - 6.0 * center
            )

    def second_plane(i, carry):
        x = 1 + i
        for c in range(comps):
            center = mid[c, x, pl.ds(top, cells_y), :]
            beside = (
                mid[c, x + 1, pl.ds(top, cells_y), :]
                + mid[c, x - 1, pl.ds(top, cells_y), :]
                + mid[c, x, pl.ds(top + 1, cells_y), :]
                + mid[c, x, pl.ds(top - 1, cells_y), :]
            )
            field = center + NU * (beside + up_down(center) - 6.0 * center)
            for h in range(chunks):
                part = field[:, h * LANES : (h + 1) * LANES]
                row = c * chunks + h
                lines[pl.ds(i * cells_y * pitch + row, cells_y, stride=pitch), :] = part
                acc[
                    pl.ds(i * cells_y * acc_pitch + row, cells_y, stride=acc_pitch), :
                ] = part
        return carry

    lax.fori_loop(0, cells_x, second_plane, 0)

    lane = lax.broadcasted_iota(jnp.int32, (LANES, LANES), 0)

    def group(zz, vv, rr, mm, local, out_row):
        for b in range(SUB):
            rows_scr[b * pitch : (b + 1) * pitch, :] = lines[
                pl.ds(pl.multiple_of(local[b] * pitch, SUB), pitch), :
            ]
        gas_rows = [
            [
                rows_scr[pl.ds(c * chunks + h, SUB, stride=pitch), :]
                for h in range(chunks)
            ]
            for c in range(comps)
        ]
        for t in range(tiles):
            part = slice(t * LANES, (t + 1) * LANES)
            pos = zz[:, part]
            low = jnp.minimum(jnp.floor(pos).astype(jnp.int32), depth - 2)
            frac = pos - low.astype(jnp.float32)
            high = low + 1
            low_chunk, low_lane = low >> 7, low & (LANES - 1)
            high_chunk, high_lane = high >> 7, high & (LANES - 1)
            relax = rr[:, part] / (1.0 + rr[:, part])
            cells_scr[:, part] = low_lane
            for c in range(comps):
                at_low = at_high = None
                for h in range(chunks):
                    got_low = jnp.take_along_axis(
                        gas_rows[c][h], low_lane, 1, mode="promise_in_bounds"
                    )
                    got_high = jnp.take_along_axis(
                        gas_rows[c][h], high_lane, 1, mode="promise_in_bounds"
                    )
                    at_low = (
                        got_low if h == 0 else jnp.where(low_chunk == h, got_low, at_low)
                    )
                    at_high = (
                        got_high
                        if h == 0
                        else jnp.where(high_chunk == h, got_high, at_high)
                    )
                gas_at = at_low * (1.0 - frac) + at_high * frac
                vel = vv[c][:, part]
                updated = vel + relax * (gas_at - vel)
                parcel_out[c, pl.ds(out_row, SUB), part] = updated
                momentum = mm[:, part] * (vel - updated)
                for w, share in enumerate((momentum * (1.0 - frac), momentum * frac)):
                    coarse = share.astype(jnp.bfloat16).astype(jnp.float32)
                    fine = share - coarse
                    for h in range(chunks):
                        row = (w * comps + c) * chunks + h
                        here = low_chunk == h
                        weights[t, row * SUB : (row + 1) * SUB, :] = jnp.where(
                            here, coarse, 0.0
                        )
                        row += half
                        weights[t, row * SUB : (row + 1) * SUB, :] = jnp.where(
                            here, fine, 0.0
                        )
        for b in range(SUB):
            spots, shares = [], []
            for t in range(tiles):
                shares.append(
                    weights[t, pl.ds(b, 2 * half, stride=SUB), :].astype(jnp.bfloat16)
                )
                cell = cells_scr[pl.ds(b, 1), t * LANES : (t + 1) * LANES]
                spots.append(
                    jnp.where(lane == cell, 1.0, 0.0).astype(jnp.bfloat16)
                )
            spot = jnp.concatenate(spots, 1)
            lhs = jnp.concatenate(shares, 1)
            both = lax.dot_general(
                lhs, spot, (((1,), (1,)), ((), ())), preferred_element_type=jnp.float32
            )
            at = pl.ds(pl.multiple_of(local[b] * acc_pitch, SUB), acc_pitch)
            acc[at, :] = acc[at, :] + (both[:half] + both[half:])

    weights[...] = jnp.zeros_like(weights)

    sub_row = lax.broadcasted_iota(jnp.int32, (SUB, width), 0)

    def staying(g, carry):
        first = pl.multiple_of(g * SUB, SUB)
        at = pl.ds(first, SUB)
        keep = jnp.zeros((SUB, width), jnp.int32)
        local = []
        for b in range(SUB):
            column = columns[first + b]
            stays = (heading_of(column, dims) == 0).astype(jnp.int32)
            keep = jnp.where(sub_row == b, stays, keep)
            local.append(local_of(column, dims))
        keep = keep == 1
        group(
            z[at, :],
            [jnp.where(keep, v[c, at, :], 0.0) for c in range(3)],
            jnp.where(keep, rate[at, :], 0.0),
            jnp.where(keep, mass[at, :], 0.0),
            local,
            first,
        )
        return carry

    lax.fori_loop(0, slots // SUB, staying, 0)

    for code in range(4):
        tails[code].wait()
        inbox = inboxes[code]

        def arriving(g, carry, code=code, inbox=inbox):
            first = pl.multiple_of(g * SUB, SUB)
            local = [
                local_of(arrived[code * SUB, first + b].astype(jnp.int32), dims)
                for b in range(SUB)
            ]
            field = [
                inbox[pl.ds(pl.multiple_of(first + f * capacity, SUB), SUB), :]
                for f in range(6)
            ]
            group(
                field[0],
                field[1:4],
                field[4],
                field[5],
                local,
                pl.multiple_of(slots + code * capacity + first, SUB),
            )
            return carry

        lax.fori_loop(0, capacity // SUB, arriving, 0)

    lane_row = lax.broadcasted_iota(jnp.int32, (cells_y, LANES), 1)

    def finish(i, carry):
        for c in range(comps):
            before = jnp.zeros((cells_y, LANES), jnp.float32)
            for h in range(chunks):
                row = c * chunks + h
                base = i * cells_y * acc_pitch + row
                low = acc[pl.ds(base, cells_y, stride=acc_pitch), :]
                high = acc[
                    pl.ds(base + comps * chunks, cells_y, stride=acc_pitch), :
                ]
                turned = pltpu.roll(high, 1, 1)
                moved = jnp.where(lane_row == 0, before, turned)
                before = turned
                gas_out[c, i, :, h * LANES : (h + 1) * LANES] = low + moved
        return carry

    lax.fori_loop(0, cells_x, finish, 0)


def neighbour(value, axis, steps):
    count = lax.axis_size(axis)
    pairs = [(source, (source + steps) % count) for source in range(count)]
    return lax.ppermute(value, axis, pairs)


def diagonal(value, x_steps, y_steps):
    groups, x_count, inner = (lax.axis_size(a) for a in ("grp", "gx", "gy"))
    y_count = groups * inner

    def flat(x, y):
        return (y // inner * x_count + x) * inner + y % inner

    pairs = [
        (flat(x, y), flat((x + x_steps) % x_count, (y + y_steps) % y_count))
        for x in range(x_count)
        for y in range(y_count)
    ]
    return lax.ppermute(value, ("grp", "gx", "gy"), pairs)


def body(gas_velocity, parcel_z, parcel_velocity, parcel_rate, parcel_mass, parcel_column):
    f32 = jnp.float32
    comps, cells_x, cells_y, depth = gas_velocity.shape
    slots, width = parcel_z.shape
    capacity = slots // 4
    x_count = lax.axis_size("gx")
    y_count = lax.axis_size(Y_AXES)
    dims = (x_count, y_count, cells_x, cells_y)
    velocity = jnp.transpose(parcel_velocity, (1, 0, 2))

    x_face = jax.ShapeDtypeStruct((comps, 2, cells_y, depth), f32)
    y_face = jax.ShapeDtypeStruct((comps, 2, cells_x, depth), f32)
    corner = jax.ShapeDtypeStruct((comps, depth), f32)
    x_up, x_down, y_up, y_down, pp, pm, mp, mm = pl.pallas_call(
        faces_kernel,
        out_shape=(x_face, x_face, y_face, y_face, corner, corner, corner, corner),
        in_specs=[VMEM],
        out_specs=(VMEM,) * 8,
        name="faces",
    )(gas_velocity)
    ll = diagonal(pp, 1, 1)
    lh = diagonal(pm, 1, -1)
    hl = diagonal(mp, -1, 1)
    hh = diagonal(mm, -1, -1)
    x_low = neighbour(x_up, "gx", 1)
    x_high = neighbour(x_down, "gx", -1)
    y_low = neighbour(y_up, Y_AXES, 1)
    y_high = neighbour(y_down, Y_AXES, -1)

    rows = 6 * capacity + SUB
    box = jax.ShapeDtypeStruct((rows, width), f32)
    outbox = pl.pallas_call(
        functools.partial(pack_kernel, dims, capacity),
        out_shape=(box,) * 4,
        in_specs=[SMEM] + [VMEM] * 4,
        out_specs=(VMEM,) * 4,
        scratch_shapes=[pltpu.VMEM((5 * rows, width), f32)],
        name="pack",
    )(parcel_column, parcel_z, velocity, parcel_rate, parcel_mass)
    inboxes = [
        neighbour(outbox[0], "gx", 1),
        neighbour(outbox[1], "gx", -1),
        neighbour(outbox[2], Y_AXES, 1),
        neighbour(outbox[3], Y_AXES, -1),
    ]

    chunks = depth // LANES
    cells = cells_x * cells_y
    pitch = -(-comps * chunks // SUB) * SUB
    acc_pitch = -(-2 * comps * chunks // SUB) * SUB
    total = slots + 4 * capacity
    gas_out, updated = pl.pallas_call(
        functools.partial(couple_kernel, dims, capacity),
        out_shape=(
            jax.ShapeDtypeStruct((comps, cells_x, cells_y, depth), f32),
            jax.ShapeDtypeStruct((3, total, width), f32),
        ),
        in_specs=[SMEM, ANY] + [VMEM] * 16,
        out_specs=(VMEM, VMEM),
        scratch_shapes=[
            pltpu.VMEM((comps, cells_x + 4, cells_y + 2 * SUB, depth), f32),
            pltpu.VMEM((comps, cells_x + 2, cells_y + 2 * SUB, depth), f32),
            pltpu.VMEM((cells * pitch, LANES), f32),
            pltpu.VMEM((cells * acc_pitch, LANES), f32),
            pltpu.VMEM((SUB * pitch, LANES), f32),
            pltpu.VMEM((width // LANES, 2 * acc_pitch * SUB, LANES), f32),
            pltpu.VMEM((SUB, width), jnp.int32),
            pltpu.SMEM((4 * SUB, LANES), f32),
            pltpu.SemaphoreType.DMA((5,)),
        ],
        name="couple",
    )(
        parcel_column,
        gas_velocity,
        x_low,
        x_high,
        y_low,
        y_high,
        ll,
        lh,
        hl,
        hh,
        parcel_z,
        velocity,
        parcel_rate,
        parcel_mass,
        *inboxes,
    )
    return gas_out, jnp.transpose(updated, (1, 0, 2))


def solution(mesh):
    placed = (
        P(None, "gx", Y_AXES, None),
        P(("grp", "gx", "gy"), None),
        P(("grp", "gx", "gy"), None, None),
        P(("grp", "gx", "gy"), None),
        P(("grp", "gx", "gy"), None),
        P(("grp", "gx", "gy")),
    )
    return jax.shard_map(
        body,
        mesh=mesh,
        in_specs=placed,
        out_specs=(P(None, "gx", Y_AXES, None), P(("grp", "gx", "gy"), None, None)),
        check_vma=False,
    )
```

time: 252 us -> 68.6 us (0.27); the launches traced: 248 us -> 68.4 us
  matrix products: 179 us -> 0 us
  Pallas kernels: 0 us -> 33.1 us
  other arithmetic: 23.6 us -> 0 us
  local copies, waits for them, and re-layouts: 24.3 us -> 1.39 us
  waiting for transfers between devices: 5.32 us -> 13.4 us
  starting transfers between devices: 14.3 us -> 19.7 us
    dot_general x26 -> x0, matrix products: 179 us -> none  [the longest x12 98.2 us: couple_group(): jnp.einsum('cbz,bpz->cbp', rows_g, hat, precision=lax.Precision.HIGHEST)]
    pallas_call x0 -> x3, Pallas kernels: none -> 33.1 us  [the longest x1 23 us: body(): pl.pallas_call(functools.partial(couple_kernel, dims, capacity), out_shap...]
    mul x12 -> x0, other arithmetic: 9 us -> none  [couple_group(): updated = velocity + relax[None] * (gas_at - velocity)]
    sub x13 -> x0, other arithmetic: 8.72 us -> none  [the longest x12 8.71 us: couple_group(): 1.0 - fraction]
    ppermute x8 -> x12, waiting for transfers between devices: 5.32 us -> 13.4 us  [the longest x8 9.36 us: neighbour(): return lax.ppermute(value, axis, pairs)]
    unnamed x10 -> x24, local copies, waits for them, and re-layouts: 8.84 us -> 1.39 us
    ppermute x8 -> x12, starting transfers between devices: 14.3 us -> 19.7 us  [the longest x8 13.4 us: neighbour(): return lax.ppermute(value, axis, pairs)]
    slice x7 -> x0, local copies, waits for them, and re-layouts: 5.27 us -> none  [the longest x1 1.73 us: with_halo(): lax.slice_in_dim(block, block.shape[dim] - width, None, axis=dim)]
  transfers between devices with their start and end apart: 8 -> 12, of which waited for: 2 -> 2; matrix products, arithmetic and copies ran while one was open for 8% -> 0% of each run, Pallas kernels for 0% -> 12%
where the time goes in v1:
time: 68.6 us; the launch traced here: 68.4 us
  Pallas kernels  33.1 us (48%)
  starting transfers between devices  19.7 us (29%)
  waiting for transfers between devices  13.4 us (20%)
  local copies, waits for them, and re-layouts  1.39 us (2%)
  between operations  0.74 us (1%)
    pallas_call x1, Pallas kernels, body(): pl.pallas_call(functools.partial(couple_kernel, dims, capacity), out_shap...  23 us
    ppermute x8, starting transfers between devices, neighbour(): return lax.ppermute(value, axis, pairs)  13.4 us
    ppermute x8, waiting for transfers between devices, neighbour(): return lax.ppermute(value, axis, pairs)  9.36 us
    pallas_call x1, Pallas kernels, body(): pl.pallas_call(functools.partial(pack_kernel, dims, capacity), out_shape=...  7.93 us
    ppermute x4, starting transfers between devices, diagonal(): return lax.ppermute(value, ('grp', 'gx', 'gy'), pairs)  6.35 us
    ppermute x4, waiting for transfers between devices, diagonal(): return lax.ppermute(value, ('grp', 'gx', 'gy'), pairs)  4.06 us
    pallas_call x1, Pallas kernels, body(): pl.pallas_call(faces_kernel, out_shape=(x_face, x_face, y_face, y_face, c...  2.12 us
    unnamed x24, local copies, waits for them, and re-layouts  1.39 us
  transfers between devices with their start and end apart: 12, of which 2 were waited for; matrix products, arithmetic and copies ran while one was open for 0% of the time, Pallas kernels for 12%

profile of v1, /device:TPU:0, one launch (start us, length us, event | category | flops | bytes accessed | tf_op | source)
XLA Modules:
  0.0 68.4 jit_solution(643250716876487040)
XLA Ops:
  0.6 2.1 %faces.1 = (f32[3,2,16,384]{3,2,1,0:T(8,128)}, f32[3,2,16,384]{3,2,1,0:T(8,128)}, f32[3,2,16,384]{3,2,1,0:T(8,128)}, f32[3,2,16,384]{3,2,1,0:T(8,128)}, f32[3,38...) custom-call(f32[3,16,16,384]{3,2,1,0:T(8,128)} %gas.3), custom_call_target="tpu_custom_call" | custom-call | tf_op jit(solution)/shard_map/faces/pallas_call | solution.py:436
  2.8 3.1 %collective-permute-start = (f32[3,2,16,384]{3,2,1,0:T(8,128)}, f32[3,2,16,384]{3,2,1,0:T(8,128)S(1)}, u32[]{:S(2)}, u32[]{:S(2)}) collective-permute-start(f32[3,2,16,384]{3,2,1,0:T(8,128)} %get-tuple-element.16), channel_id=1, source_target_pairs={{0,4},{4,8},{8,12},{12,0},{1,5},{5,9},{9,13},{13,1},{2,6},{6,10},{... | collective-permute-start | bytes 442376 | tf_op jit(solution)/shard_map/ppermute | solution.py:405
  5.8 2.1 %collective-permute-start.1 = (f32[3,2,16,384]{3,2,1,0:T(8,128)}, f32[3,2,16,384]{3,2,1,0:T(8,128)S(1)}, u32[]{:S(2)}, u32[]{:S(2)}) collective-permute-start(f32[3,2,16,384]{3,2,1,0:T(8,128)} %get-tuple-element.17), channel_id=1, source_target_pairs={{0,12},{4,0},{8,4},{12,8},{1,13},{5,1},{9,5},{13,9},{2,14},{6,2},{... | collective-permute-start | bytes 442376 | tf_op jit(solution)/shard_map/ppermute | solution.py:405
  7.9 1.7 %collective-permute-start.2 = (f32[3,2,16,384]{3,2,1,0:T(8,128)}, f32[3,2,16,384]{3,2,1,0:T(8,128)S(1)}, u32[]{:S(2)}, u32[]{:S(2)}) collective-permute-start(f32[3,2,16,384]{3,2,1,0:T(8,128)} %get-tuple-element.18), channel_id=1, source_target_pairs={{0,1},{1,2},{2,3},{3,16},{16,17},{17,18},{18,19},{19,0},{4,5},{5,6... | collective-permute-start | bytes 442376 | tf_op jit(solution)/shard_map/ppermute | solution.py:405
  9.5 0.7 %collective-permute-start.4 = (f32[3,384]{1,0:T(4,128)}, f32[3,384]{1,0:T(4,128)S(1)}, u32[]{:S(2)}, u32[]{:S(2)}) collective-permute-start(f32[3,384]{1,0:T(4,128)} %get-tuple-element.20), channel_id=1, source_target_pairs={{0,5},{1,6},{2,7},{3,20},{16,21},{17,22},{18,23},{19,4},{4,9},{5,1... | collective-permute-start | bytes 13832 | tf_op jit(solution)/shard_map/ppermute | solution.py:420
  10.2 2.2 %collective-permute-start.5 = (f32[3,384]{1,0:T(4,128)}, f32[3,384]{1,0:T(4,128)S(1)}, u32[]{:S(2)}, u32[]{:S(2)}) collective-permute-start(f32[3,384]{1,0:T(4,128)} %get-tuple-element.21), channel_id=1, source_target_pairs={{0,23},{1,4},{2,5},{3,6},{16,7},{17,20},{18,21},{19,22},{4,27},{5,... | collective-permute-start | bytes 13832 | tf_op jit(solution)/shard_map/ppermute | solution.py:420
  12.4 4.0 %collective-permute-done.4.ll = f32[3,384]{1,0:T(4,128)S(1)} collective-permute-done((f32[3,384]{1,0:T(4,128)}, f32[3,384]{1,0:T(4,128)S(1)}, u32[]{:S(2)}, u32[]{:S(2)}) %collective-permute-start.4) | collective-permute-done | bytes 4640 | tf_op jit(solution)/shard_map/ppermute | solution.py:420
  16.5 1.4 %collective-permute-start.6 = (f32[3,384]{1,0:T(4,128)}, f32[3,384]{1,0:T(4,128)S(1)}, u32[]{:S(2)}, u32[]{:S(2)}) collective-permute-start(f32[3,384]{1,0:T(4,128)} %get-tuple-element.22), channel_id=1, source_target_pairs={{0,13},{1,14},{2,15},{3,28},{16,29},{17,30},{18,31},{19,12},{4,1},... | collective-permute-start | bytes 13832 | tf_op jit(solution)/shard_map/ppermute | solution.py:420
  17.8 0.0 collective-permute-done.5.lh
  17.8 2.1 %collective-permute-start.7 = (f32[3,384]{1,0:T(4,128)}, f32[3,384]{1,0:T(4,128)S(1)}, u32[]{:S(2)}, u32[]{:S(2)}) collective-permute-start(f32[3,384]{1,0:T(4,128)} %get-tuple-element.23), channel_id=1, source_target_pairs={{0,31},{1,12},{2,13},{3,14},{16,15},{17,28},{18,29},{19,30},{4,19}... | collective-permute-start | bytes 13832 | tf_op jit(solution)/shard_map/ppermute | solution.py:420
  20.0 7.9 %pack.1 = (f32[152,256]{1,0:T(8,128)}, f32[152,256]{1,0:T(8,128)}, f32[152,256]{1,0:T(8,128)}, f32[152,256]{1,0:T(8,128)}) custom-call(s32[96]{0:T(128)} %columns.3, f32[96,256]{1,0:T(8,128)} %z.3, f32[3,96,256]{2,1,0:T(8,128)} %bitcast.2, f32[96,256]{1,0:T(8,128)} %rate.3, f32[96,256]{1,0:T(8,128)} %mass.3), custom_call_target="tpu_custom_call" | custom-call | tf_op jit(solution)/shard_map/pack/pallas_call | solution.py:454
  27.9 0.0 collective-permute-done.6.hl
  27.9 1.2 %collective-permute-start.8 = (f32[152,256]{1,0:T(8,128)}, f32[152,256]{1,0:T(8,128)S(1)}, u32[]{:S(2)}, u32[]{:S(2)}) collective-permute-start(f32[152,256]{1,0:T(8,128)} %get-tuple-element.24), channel_id=1, source_target_pairs={{0,4},{4,8},{8,12},{12,0},{1,5},{5,9},{9,13},{13,1},{2,6},{6,10},{... | collective-permute-start | bytes 466952 | tf_op jit(solution)/shard_map/ppermute | solution.py:405
  29.1 0.0 collective-permute-done.7.hh
  29.1 2.7 %collective-permute-start.9 = (f32[152,256]{1,0:T(8,128)}, f32[152,256]{1,0:T(8,128)S(1)}, u32[]{:S(2)}, u32[]{:S(2)}) collective-permute-start(f32[152,256]{1,0:T(8,128)} %get-tuple-element.25), channel_id=1, source_target_pairs={{0,12},{4,0},{8,4},{12,8},{1,13},{5,1},{9,5},{13,9},{2,14},{6,2},{... | collective-permute-start | bytes 466952 | tf_op jit(solution)/shard_map/ppermute | solution.py:405
  31.8 0.0 collective-permute-done.x_low
  31.8 0.5 collective-permute-start.10
  32.3 0.0 collective-permute-done.1.x_high
  32.3 2.1 %collective-permute-start.11 = (f32[152,256]{1,0:T(8,128)}, f32[152,256]{1,0:T(8,128)S(1)}, u32[]{:S(2)}, u32[]{:S(2)}) collective-permute-start(f32[152,256]{1,0:T(8,128)} %get-tuple-element.27), channel_id=1, source_target_pairs={{0,19},{1,0},{2,1},{3,2},{16,3},{17,16},{18,17},{19,18},{4,23},{5,... | collective-permute-start | bytes 466952 | tf_op jit(solution)/shard_map/ppermute | solution.py:405
  34.4 0.0 collective-permute-done.2.y_low
  34.4 0.1 collective-permute-start.3
  34.5 9.3 %collective-permute-done.3.y_high = f32[3,2,16,384]{3,2,1,0:T(8,128)S(1)} collective-permute-done((f32[3,2,16,384]{3,2,1,0:T(8,128)}, f32[3,2,16,384]{3,2,1,0:T(8,128)S(1)}, u32[]{:S(2)}, u32[]{:S(2)}) %collective-permute-start.3) | collective-permute-done | bytes 147488 | tf_op jit(solution)/shard_map/ppermute | solution.py:405
  43.9 0.0 collective-permute-done.8.in0
  43.9 0.0 collective-permute-done.9.in1
  43.9 0.0 collective-permute-done.10.in2
  43.9 0.0 collective-permute-done.11.in3
  44.0 0.5 copy-done.7
  44.5 0.1 copy-done
  44.6 0.1 copy-done.1
  44.6 0.0 copy-done.2
  44.7 0.7 copy-done.3
  45.3 23.0 %couple.1 = (f32[3,16,16,384]{3,2,1,0:T(8,128)}, f32[3,192,256]{2,1,0:T(8,128)}) custom-call(s32[96]{0:T(128)} %columns.3, f32[3,16,16,384]{3,2,1,0:T(8,128)} %gas.3, f32[3,2,16,384]{3,2,1,0:T(8,128)} %copy-done.4, f32[3,2,16,384]{3,2,1,0:T(8,128)} %copy-done.5, f32[3,2,16,384]{3,2,1,0:T(8,128)} %copy-done.6, f32[3,2,16,384]{3,2,1,0:T(8,128)} %copy-done.7, ...), custom_call_target="tpu_custom_call" | custom-call | tf_op jit(solution)/shard_map/couple/pallas_call | solution.py:474
  (19 shorter events, 0.0 us)
Async XLA Ops:
  2.8 29.0 %collective-permute-start = (f32[3,2,16,384]{3,2,1,0:T(8,128)}, f32[3,2,16,384]{3,2,1,0:T(8,128)S(1)}, u32[]{:S(2)}, u32[]{:S(2)}) collective-permute-start(f32[3,2,16,384]{3,2,1,0:T(8,128)} %get-tuple-element.16), channel_id=1, source_target_pairs={{0,4},{4,8},{8,12},{12,0},{1,5},{5,9},{9,13},{13,1},{2,6},{6,10},{... | collective-permute-start | bytes 442376 | tf_op jit(solution)/shard_map/ppermute | solution.py:405
  5.8 26.5 %collective-permute-start.1 = (f32[3,2,16,384]{3,2,1,0:T(8,128)}, f32[3,2,16,384]{3,2,1,0:T(8,128)S(1)}, u32[]{:S(2)}, u32[]{:S(2)}) collective-permute-start(f32[3,2,16,384]{3,2,1,0:T(8,128)} %get-tuple-element.17), channel_id=1, source_target_pairs={{0,12},{4,0},{8,4},{12,8},{1,13},{5,1},{9,5},{13,9},{2,14},{6,2},{... | collective-permute-start | bytes 442376 | tf_op jit(solution)/shard_map/ppermute | solution.py:405
  7.9 26.6 %collective-permute-start.2 = (f32[3,2,16,384]{3,2,1,0:T(8,128)}, f32[3,2,16,384]{3,2,1,0:T(8,128)S(1)}, u32[]{:S(2)}, u32[]{:S(2)}) collective-permute-start(f32[3,2,16,384]{3,2,1,0:T(8,128)} %get-tuple-element.18), channel_id=1, source_target_pairs={{0,1},{1,2},{2,3},{3,16},{16,17},{17,18},{18,19},{19,0},{4,5},{5,6... | collective-permute-start | bytes 442376 | tf_op jit(solution)/shard_map/ppermute | solution.py:405
  9.5 6.9 %collective-permute-start.4 = (f32[3,384]{1,0:T(4,128)}, f32[3,384]{1,0:T(4,128)S(1)}, u32[]{:S(2)}, u32[]{:S(2)}) collective-permute-start(f32[3,384]{1,0:T(4,128)} %get-tuple-element.20), channel_id=1, source_target_pairs={{0,5},{1,6},{2,7},{3,20},{16,21},{17,22},{18,23},{19,4},{4,9},{5,1... | collective-permute-start | bytes 13832 | tf_op jit(solution)/shard_map/ppermute | solution.py:420
  10.2 7.6 %collective-permute-start.5 = (f32[3,384]{1,0:T(4,128)}, f32[3,384]{1,0:T(4,128)S(1)}, u32[]{:S(2)}, u32[]{:S(2)}) collective-permute-start(f32[3,384]{1,0:T(4,128)} %get-tuple-element.21), channel_id=1, source_target_pairs={{0,23},{1,4},{2,5},{3,6},{16,7},{17,20},{18,21},{19,22},{4,27},{5,... | collective-permute-start | bytes 13832 | tf_op jit(solution)/shard_map/ppermute | solution.py:420
  16.5 27.5 %copy-start.8 = (f32[3,384]{1,0:T(4,128)}, f32[3,384]{1,0:T(4,128)S(1)}, u32[]{:S(2)}) copy-start(f32[3,384]{1,0:T(4,128)S(1)} %collective-permute-done.4.ll) | copy-start | bytes 13828
  16.5 11.4 %collective-permute-start.6 = (f32[3,384]{1,0:T(4,128)}, f32[3,384]{1,0:T(4,128)S(1)}, u32[]{:S(2)}, u32[]{:S(2)}) collective-permute-start(f32[3,384]{1,0:T(4,128)} %get-tuple-element.22), channel_id=1, source_target_pairs={{0,13},{1,14},{2,15},{3,28},{16,29},{17,30},{18,31},{19,12},{4,1},... | collective-permute-start | bytes 13832 | tf_op jit(solution)/shard_map/ppermute | solution.py:420
  17.8 26.1 %copy-start.9 = (f32[3,384]{1,0:T(4,128)}, f32[3,384]{1,0:T(4,128)S(1)}, u32[]{:S(2)}) copy-start(f32[3,384]{1,0:T(4,128)S(1)} %collective-permute-done.5.lh) | copy-start | bytes 13828
  17.8 11.3 %collective-permute-start.7 = (f32[3,384]{1,0:T(4,128)}, f32[3,384]{1,0:T(4,128)S(1)}, u32[]{:S(2)}, u32[]{:S(2)}) collective-permute-start(f32[3,384]{1,0:T(4,128)} %get-tuple-element.23), channel_id=1, source_target_pairs={{0,31},{1,12},{2,13},{3,14},{16,15},{17,28},{18,29},{19,30},{4,19}... | collective-permute-start | bytes 13832 | tf_op jit(solution)/shard_map/ppermute | solution.py:420
  27.9 16.1 %copy-start.10 = (f32[3,384]{1,0:T(4,128)}, f32[3,384]{1,0:T(4,128)S(1)}, u32[]{:S(2)}) copy-start(f32[3,384]{1,0:T(4,128)S(1)} %collective-permute-done.6.hl) | copy-start | bytes 13828
  27.9 16.0 %collective-permute-start.8 = (f32[152,256]{1,0:T(8,128)}, f32[152,256]{1,0:T(8,128)S(1)}, u32[]{:S(2)}, u32[]{:S(2)}) collective-permute-start(f32[152,256]{1,0:T(8,128)} %get-tuple-element.24), channel_id=1, source_target_pairs={{0,4},{4,8},{8,12},{12,0},{1,5},{5,9},{9,13},{13,1},{2,6},{6,10},{... | collective-permute-start | bytes 466952 | tf_op jit(solution)/shard_map/ppermute | solution.py:405
  29.1 14.8 %copy-start.11 = (f32[3,384]{1,0:T(4,128)}, f32[3,384]{1,0:T(4,128)S(1)}, u32[]{:S(2)}) copy-start(f32[3,384]{1,0:T(4,128)S(1)} %collective-permute-done.7.hh) | copy-start | bytes 13828
  29.1 14.8 %collective-permute-start.9 = (f32[152,256]{1,0:T(8,128)}, f32[152,256]{1,0:T(8,128)S(1)}, u32[]{:S(2)}, u32[]{:S(2)}) collective-permute-start(f32[152,256]{1,0:T(8,128)} %get-tuple-element.25), channel_id=1, source_target_pairs={{0,12},{4,0},{8,4},{12,8},{1,13},{5,1},{9,5},{13,9},{2,14},{6,2},{... | collective-permute-start | bytes 466952 | tf_op jit(solution)/shard_map/ppermute | solution.py:405
  31.8 12.2 %copy-start.4 = (f32[3,2,16,384]{3,2,1,0:T(8,128)}, f32[3,2,16,384]{3,2,1,0:T(8,128)S(1)}, u32[]{:S(2)}) copy-start(f32[3,2,16,384]{3,2,1,0:T(8,128)S(1)} %collective-permute-done.x_low) | copy-start | bytes 442372
  31.8 12.1 %collective-permute-start.10 = (f32[152,256]{1,0:T(8,128)}, f32[152,256]{1,0:T(8,128)S(1)}, u32[]{:S(2)}, u32[]{:S(2)}) collective-permute-start(f32[152,256]{1,0:T(8,128)} %get-tuple-element.26), channel_id=1, source_target_pairs={{0,1},{1,2},{2,3},{3,16},{16,17},{17,18},{18,19},{19,0},{4,5},{5,6... | collective-permute-start | bytes 466952 | tf_op jit(solution)/shard_map/ppermute | solution.py:405
  32.3 11.6 %copy-start.5 = (f32[3,2,16,384]{3,2,1,0:T(8,128)}, f32[3,2,16,384]{3,2,1,0:T(8,128)S(1)}, u32[]{:S(2)}) copy-start(f32[3,2,16,384]{3,2,1,0:T(8,128)S(1)} %collective-permute-done.1.x_high) | copy-start | bytes 442372
  32.3 11.6 %collective-permute-start.11 = (f32[152,256]{1,0:T(8,128)}, f32[152,256]{1,0:T(8,128)S(1)}, u32[]{:S(2)}, u32[]{:S(2)}) collective-permute-start(f32[152,256]{1,0:T(8,128)} %get-tuple-element.27), channel_id=1, source_target_pairs={{0,19},{1,0},{2,1},{3,2},{16,3},{17,16},{18,17},{19,18},{4,23},{5,... | collective-permute-start | bytes 466952 | tf_op jit(solution)/shard_map/ppermute | solution.py:405
  34.4 9.5 %copy-start.6 = (f32[3,2,16,384]{3,2,1,0:T(8,128)}, f32[3,2,16,384]{3,2,1,0:T(8,128)S(1)}, u32[]{:S(2)}) copy-start(f32[3,2,16,384]{3,2,1,0:T(8,128)S(1)} %collective-permute-done.2.y_low) | copy-start | bytes 442372
  34.4 9.4 %collective-permute-start.3 = (f32[3,2,16,384]{3,2,1,0:T(8,128)}, f32[3,2,16,384]{3,2,1,0:T(8,128)S(1)}, u32[]{:S(2)}, u32[]{:S(2)}) collective-permute-start(f32[3,2,16,384]{3,2,1,0:T(8,128)} %get-tuple-element.19), channel_id=1, source_target_pairs={{0,19},{1,0},{2,1},{3,2},{16,3},{17,16},{18,17},{19,18},{4,23},{5,... | collective-permute-start | bytes 442376 | tf_op jit(solution)/shard_map/ppermute | solution.py:405
  43.9 0.7 copy-start.7
  43.9 0.7 %copy-start = (f32[152,256]{1,0:T(8,128)}, f32[152,256]{1,0:T(8,128)S(1)}, u32[]{:S(2)}) copy-start(f32[152,256]{1,0:T(8,128)S(1)} %collective-permute-done.8.in0) | copy-start | bytes 466948
  43.9 0.8 %copy-start.1 = (f32[152,256]{1,0:T(8,128)}, f32[152,256]{1,0:T(8,128)S(1)}, u32[]{:S(2)}) copy-start(f32[152,256]{1,0:T(8,128)S(1)} %collective-permute-done.9.in1) | copy-start | bytes 466948
  43.9 0.8 %copy-start.2 = (f32[152,256]{1,0:T(8,128)}, f32[152,256]{1,0:T(8,128)S(1)}, u32[]{:S(2)}) copy-start(f32[152,256]{1,0:T(8,128)S(1)} %collective-permute-done.10.in2) | copy-start | bytes 466948
  44.7 0.7 copy-start.3

commit v2 on v0

v2 whole, which is shorter than its diff:
```python
import functools

import jax
import jax.numpy as jnp
from jax import lax
from jax.experimental import pallas as pl
from jax.experimental.pallas import tpu as pltpu
from jax.sharding import PartitionSpec as P


NU = 0.1
LANES = 128
SUB = 8
UNROLL = 3
FIELDS = 6
Y_AXES = ("grp", "gy")
F32 = jnp.float32
BF16 = jnp.bfloat16

VMEM = pl.BlockSpec(memory_space=pltpu.VMEM)
SMEM = pl.BlockSpec(memory_space=pltpu.SMEM)
HBM = pl.BlockSpec(memory_space=pltpu.HBM)


def quotient(value, by):
    if by & (by - 1) == 0:
        return value >> (by.bit_length() - 1)
    return lax.div(value, jnp.full_like(value, by))


def remainder(value, by):
    if by & (by - 1) == 0:
        return value & (by - 1)
    return lax.rem(value, jnp.full_like(value, by))


def y_place():
    return lax.axis_index("grp") * lax.axis_size("gy") + lax.axis_index("gy")


def heading_of(column, dims):
    x_count, y_count, cells_x, cells_y = dims
    rows_total = cells_y * y_count
    x_index, y_index = lax.axis_index("gx"), y_place()
    target_x = quotient(column, rows_total * cells_x)
    target_y = quotient(remainder(column, rows_total), cells_y)
    x_up, x_down = lax.rem(x_index + 1, x_count), lax.rem(x_index + x_count - 1, x_count)
    y_up, y_down = lax.rem(y_index + 1, y_count), lax.rem(y_index + y_count - 1, y_count)
    return jnp.where(
        target_x == x_up,
        1,
        jnp.where(
            target_x == x_down,
            2,
            jnp.where(target_y == y_up, 3, jnp.where(target_y == y_down, 4, 0)),
        ),
    )


def local_of(column, dims):
    _, y_count, cells_x, cells_y = dims
    x = remainder(quotient(column, cells_y * y_count), cells_x)
    return x * cells_y + remainder(column, cells_y)


def faces_kernel(gas, z, v, rate, mass, x_up, x_down, y_up, y_down, ext, state, sems):
    comps, cells_x, cells_y, depth = gas.shape
    chunks = depth // LANES
    copies = [
        pltpu.make_async_copy(
            gas.at[:, :, :, pl.ds(h * LANES, LANES)],
            ext.at[:, h, pl.ds(2, cells_x), pl.ds(SUB, cells_y), :],
            sems.at[h],
        )
        for h in range(chunks)
    ]
    for i, (source, target) in enumerate(
        (
            (z, state.at[0]),
            (v, state.at[pl.ds(1, 3)]),
            (rate, state.at[4]),
            (mass, state.at[5]),
        )
    ):
        copies.append(pltpu.make_async_copy(source, target, sems.at[chunks + i]))
    for copy in copies:
        copy.start()
    rows = pl.ds(SUB, cells_y)
    for h in range(chunks):
        copies[h].wait()
        for c in range(comps):
            for near in range(2):
                x_up[c, h, near] = ext[c, h, cells_x + near, rows, :]
                x_down[c, h, near] = ext[c, h, 2 + near, rows, :]
                planes = pl.ds(2, cells_x)
                y_up[c, h, near] = ext[c, h, planes, SUB + cells_y - 2 + near, :]
                y_down[c, h, near] = ext[c, h, planes, SUB + near, :]
    for copy in copies[chunks:]:
        copy.wait()


def pack_kernel(dims, capacity, columns, state, box0, box1, box2, box3, keep):
    boxes = (box0, box1, box2, box3)
    _, slots, _ = state.shape
    column = columns[...]
    head = heading_of(column, dims)
    code = lax.broadcasted_iota(jnp.int32, (SUB, slots), 0) + 1
    leaves = jnp.where((code == head) & (code <= 4), 1.0, 0.0)
    before = jnp.where(
        lax.broadcasted_iota(jnp.int32, (slots, slots), 0)
        < lax.broadcasted_iota(jnp.int32, (slots, slots), 1),
        1.0,
        0.0,
    )
    ranks = jnp.dot(
        leaves.astype(BF16), before.astype(BF16), preferred_element_type=F32
    )
    rank = jnp.sum(ranks * leaves, 0, keepdims=True).astype(jnp.int32)
    target = jnp.where(
        (head > 0) & (rank < capacity), (head - 1) * capacity + rank, -1
    )
    select = jnp.where(
        lax.broadcasted_iota(jnp.int32, (4 * capacity, slots), 0) == target, 1.0, 0.0
    ).astype(BF16)
    for f in range(FIELDS):
        whole = state[f]
        first = whole.astype(BF16)
        rest = whole - first.astype(F32)
        second = rest.astype(BF16)
        third = (rest - second.astype(F32)).astype(BF16)
        moved = (
            jnp.dot(select, first, preferred_element_type=F32)
            + jnp.dot(select, second, preferred_element_type=F32)
        ) + jnp.dot(select, third, preferred_element_type=F32)
        for d in range(4):
            boxes[d][f * capacity : (f + 1) * capacity, :] = moved[
                d * capacity : (d + 1) * capacity
            ]
    digit = lax.broadcasted_iota(jnp.int32, (SUB, slots), 0)
    digits = jnp.where(
        digit == 0,
        column & 255,
        jnp.where(
            digit == 1, (column >> 8) & 255, jnp.where(digit == 2, column >> 16, 0)
        ),
    )
    found = lax.dot_general(
        digits.astype(F32).astype(BF16),
        select,
        (((1,), (1,)), ((), ())),
        preferred_element_type=F32,
    )
    same = lax.broadcasted_iota(jnp.int32, (slots, slots), 0)
    same = same == lax.broadcasted_iota(jnp.int32, (slots, slots), 1)
    keep[...] = jnp.dot(
        jnp.where(same & (head == 0), 1.0, 0.0).astype(BF16),
        jnp.ones((slots, LANES), BF16),
        preferred_element_type=F32,
    )
    tail = found[0:1] + 256.0 * found[1:2] + 65536.0 * found[2:3]
    for d in range(4):
        boxes[d][FIELDS * capacity : FIELDS * capacity + 1, 0 : 4 * capacity] = tail


def relay_kernel(x_low, x_high, box2, box3, up, down, out2, out3):
    del box2, box3, out2, out3
    comps, chunks, _, cells_y, _ = x_low.shape
    for side, (face, near) in enumerate(((x_low, 1), (x_high, 0))):
        for c in range(comps):
            for h in range(chunks):
                row = pl.ds((side * comps + c) * chunks + h, 1)
                up[row, :] = face[c, h, near, pl.ds(cells_y - 1, 1), :]
                down[row, :] = face[c, h, near, pl.ds(0, 1), :]


def stage_one(space, u, zz, vv, rr, mm, local, store):
    lines, rows_scr, shares, marks, comps, chunks = space
    steps = rows_scr.shape[1]
    for b in range(SUB):
        for k in range(steps):
            at = pl.multiple_of((local[b] * steps + k) * SUB, SUB)
            rows_scr[u, k, b * SUB : (b + 1) * SUB, :] = lines[pl.ds(at, SUB), :]
    gas_rows = [
        rows_scr[u, r // SUB, pl.ds(r % SUB, SUB, stride=SUB), :]
        for r in range(comps * chunks)
    ]
    top_cell = chunks * LANES - 2
    for t in range(zz.shape[1] // LANES):
        part = slice(t * LANES, (t + 1) * LANES)
        pos = zz[:, part]
        low = jnp.minimum(jnp.floor(pos).astype(jnp.int32), top_cell)
        frac = pos - low.astype(F32)
        high = low + 1
        low_chunk, low_lane = low >> 7, low & (LANES - 1)
        high_chunk, high_lane = high >> 7, high & (LANES - 1)
        relax = rr[:, part] / (1.0 + rr[:, part])
        marks[u, t, 0:SUB, :] = low_lane.astype(F32)
        marks[u, t, SUB : 2 * SUB, :] = low_chunk.astype(F32)
        for c in range(comps):
            at_low = at_high = None
            for h in range(chunks):
                row = gas_rows[c * chunks + h]
                got_low = jnp.take_along_axis(
                    row, low_lane, 1, mode="promise_in_bounds"
                )
                got_high = jnp.take_along_axis(
                    row, high_lane, 1, mode="promise_in_bounds"
                )
                at_low = got_low if h == 0 else jnp.where(low_chunk == h, got_low, at_low)
                at_high = (
                    got_high if h == 0 else jnp.where(high_chunk == h, got_high, at_high)
                )
            gas_at = at_low * (1.0 - frac) + at_high * frac
            vel = vv[c][:, part]
            updated = vel + relax * (gas_at - vel)
            store(c, part, updated)
            momentum = mm[:, part] * (vel - updated)
            for w, share in enumerate((momentum * (1.0 - frac), momentum * frac)):
                coarse = share.astype(BF16).astype(F32)
                row = (w * comps + c) * SUB
                shares[u, t, row : row + SUB, :] = coarse
                row += SUB * SUB
                shares[u, t, row : row + SUB, :] = share - coarse


def stage_two(space, acc, u, local, tiles):
    _, _, shares, marks, _, chunks = space
    pack = 2 * SUB
    place = lax.broadcasted_iota(jnp.int32, (pack, LANES), 0).astype(F32).astype(BF16)
    one, none = BF16(1.0), BF16(0.0)
    for b in range(SUB):
        spots, parts = [], []
        for t in range(tiles):
            share = shares[u, t, pl.ds(b, pack, stride=SUB), :].astype(BF16)
            lane = jnp.broadcast_to(marks[u, t, pl.ds(b, 1), :], (pack, LANES))
            chunk = jnp.broadcast_to(marks[u, t, pl.ds(SUB + b, 1), :], (pack, LANES))
            offset = lane.astype(BF16) - place
            chunk = chunk.astype(BF16)
            parts.append(
                jnp.concatenate(
                    [
                        jnp.where(chunk == BF16(h), share, none)
                        for h in range(chunks)
                    ],
                    0,
                )
            )
            spots.append(
                jnp.concatenate(
                    [
                        jnp.where(offset == BF16(pack * i), one, none)
                        for i in range(LANES // pack)
                    ],
                    0,
                )
            )
        both = lax.dot_general(
            jnp.concatenate(parts, 1),
            jnp.concatenate(spots, 1),
            (((1,), (1,)), ((), ())),
            preferred_element_type=F32,
        )
        for h in range(chunks):
            at = pl.ds(pl.multiple_of((local[b] * chunks + h) * SUB, SUB), SUB)
            row = h * pack
            acc[at, :] = acc[at, :] + (
                both[row : row + SUB] + both[row + SUB : row + pack]
            )


def mixed(center, x_next, x_last, y_next, y_last):
    chunks = len(center)
    lane = lax.broadcasted_iota(jnp.int32, center[0].shape, 1)
    ups = [pltpu.roll(value, LANES - 1, 1) for value in center] + [0.0]
    downs = [0.0] + [pltpu.roll(value, 1, 1) for value in center]
    result = []
    for h in range(chunks):
        above = jnp.where(lane == LANES - 1, ups[h + 1], ups[h])
        below = jnp.where(lane == 0, downs[h], downs[h + 1])
        around = ((x_next[h] + x_last[h]) + (y_next[h] + y_last[h])) + (above + below)
        result.append(center[h] * (1.0 - 6.0 * NU) + NU * around)
    return result


def stay_kernel(
    dims,
    columns,
    ext_in,
    x_low,
    x_high,
    y_low,
    y_high,
    corner_low,
    corner_high,
    state,
    keep,
    lines,
    acc,
    stayed,
    field,
    ext,
    mid,
    rows_scr,
    shares,
    marks,
):
    del ext_in
    _, _, cells_x, cells_y = dims
    comps, chunks = field.shape[:2]
    _, slots, width = state.shape
    top = SUB
    rows = pl.ds(top, cells_y)
    steps = rows_scr.shape[1]
    pitch = steps * SUB
    acc[...] = jnp.zeros_like(acc)

    planes = pl.ds(2, cells_x)
    for c in range(comps):
        for h in range(chunks):
            ext[c, h, 0:2, rows, :] = x_low[c, h]
            ext[c, h, 2 + cells_x : 4 + cells_x, rows, :] = x_high[c, h]
            ext[c, h, planes, top - 1, :] = y_low[c, h, 1]
            ext[c, h, planes, top + cells_y, :] = y_high[c, h, 0]
            for corner, y in ((corner_low, top - 1), (corner_high, top + cells_y)):
                for side, x in ((0, 1), (1, 2 + cells_x)):
                    line = corner[pl.ds((side * comps + c) * chunks + h, 1), :]
                    ext[c, h, x, pl.ds(y, 1), :] = line

    def plane(source, c, x):
        return mixed(
            *(
                [source[c, h, x + dx, pl.ds(top + dy, cells_y), :] for h in range(chunks)]
                for dx, dy in ((0, 0), (1, 0), (-1, 0), (0, 1), (0, -1))
            )
        )

    def first_plane(i, carry):
        for c in range(comps):
            for h, value in enumerate(plane(ext, c, 1 + i)):
                mid[c, h, i, rows, :] = value
        return carry

    lax.fori_loop(0, cells_x + 2, first_plane, 0)

    x_row = lax.broadcasted_iota(jnp.int32, (cells_x, LANES), 0)
    for c in range(comps):
        for face, near, far, inner, corner, row in (
            (y_low, 1, 0, top, corner_low, top - 1),
            (y_high, 0, 1, top + cells_y - 1, corner_high, top + cells_y),
        ):
            center = [face[c, h, near] for h in range(chunks)]
            left, right = [], []
            for h in range(chunks):
                first = corner[pl.ds(c * chunks + h, 1), :]
                last = corner[pl.ds((comps + c) * chunks + h, 1), :]
                left.append(jnp.where(x_row == 0, first, pltpu.roll(center[h], 1, 0)))
                right.append(
                    jnp.where(
                        x_row == cells_x - 1,
                        last,
                        pltpu.roll(center[h], cells_x - 1, 0),
                    )
                )
            outer = [face[c, h, far] for h in range(chunks)]
            inside = [ext[c, h, planes, inner, :] for h in range(chunks)]
            for h, value in enumerate(mixed(center, left, right, outer, inside)):
                mid[c, h, pl.ds(1, cells_x), row, :] = value

    def second_plane(i, carry):
        for c in range(comps):
            for h, value in enumerate(plane(mid, c, 1 + i)):
                field[c, h, i] = value
                at = i * cells_y * pitch + c * chunks + h
                lines[pl.ds(at, cells_y, stride=pitch), :] = value
        return carry

    lax.fori_loop(0, cells_x, second_plane, 0)

    space = (lines, rows_scr, shares, marks, comps, chunks)

    def staying(g, carry):
        locals_of = []
        for u in range(UNROLL):
            first = pl.multiple_of((g * UNROLL + u) * SUB, SUB)
            at = pl.ds(first, SUB)
            stays = jnp.tile(keep[at, :], (1, width // LANES)) > 0.0
            local = [local_of(columns[first + b], dims) for b in range(SUB)]
            locals_of.append(local)

            def store(c, part, value, at=at):
                stayed[c, at, part] = value

            stage_one(
                space,
                u,
                state[0, at, :],
                [jnp.where(stays, state[1 + c, at, :], 0.0) for c in range(3)],
                jnp.where(stays, state[4, at, :], 0.0),
                jnp.where(stays, state[5, at, :], 0.0),
                local,
                store,
            )
        for u in range(UNROLL):
            stage_two(space, acc, u, locals_of[u], width // LANES)
        return carry

    lax.fori_loop(0, slots // SUB // UNROLL, staying, 0)


def arrive_kernel(
    dims,
    capacity,
    in0,
    in1,
    in2,
    in3,
    lines,
    acc_in,
    stayed,
    field,
    gas_out,
    parcel_out,
    acc,
    gas_new,
    parcel_new,
    rows_scr,
    shares,
    marks,
    arrived,
    sems,
    plane_sems,
):
    del acc_in
    _, _, cells_x, cells_y = dims
    comps, chunks = field.shape[:2]
    _, slots, width = stayed.shape
    inboxes = (in0, in1, in2, in3)
    tails = [
        pltpu.make_async_copy(
            inboxes[d].at[pl.ds(FIELDS * capacity, SUB), pl.ds(0, LANES)],
            arrived.at[pl.ds(d * SUB, SUB), :],
            sems.at[d],
        )
        for d in range(4)
    ]
    for tail in tails:
        tail.start()
    kept = pltpu.make_async_copy(
        stayed, parcel_out.at[:, pl.ds(0, slots), :], sems.at[4]
    )
    kept.start()
    space = (lines, rows_scr, shares, marks, comps, chunks)
    for tail in tails:
        tail.wait()
    for d in range(4):
        inbox = inboxes[d]
        for start in range(0, capacity // SUB, UNROLL):
            groups = range(start, min(start + UNROLL, capacity // SUB))
            locals_of = []
            for u, g in enumerate(groups):
                first = g * SUB
                local = [
                    local_of(
                        arrived[d * SUB, d * capacity + first + b].astype(jnp.int32),
                        dims,
                    )
                    for b in range(SUB)
                ]
                locals_of.append(local)
                values = [
                    inbox[first + f * capacity : first + f * capacity + SUB, :]
                    for f in range(FIELDS)
                ]
                row = d * capacity + first

                def store(c, part, value, row=row):
                    parcel_new[c, row : row + SUB, part] = value

                stage_one(
                    space, u, values[0], values[1:4], values[4], values[5], local, store
                )
            for u, _ in enumerate(groups):
                stage_two(space, acc, u, locals_of[u], width // LANES)
    fresh = pltpu.make_async_copy(
        parcel_new, parcel_out.at[:, pl.ds(slots, 4 * capacity), :], sems.at[5]
    )
    fresh.start()

    lane_row = lax.broadcasted_iota(jnp.int32, (cells_y, LANES), 1)
    pitch = chunks * SUB

    def finish(i, carry):
        for c in range(comps):
            before = jnp.zeros((cells_y, LANES), F32)
            for h in range(chunks):
                base = i * cells_y * pitch + h * SUB + c
                low = acc[pl.ds(base, cells_y, stride=pitch), :]
                high = acc[pl.ds(base + comps, cells_y, stride=pitch), :]
                turned = pltpu.roll(high, 1, 1)
                moved = jnp.where(lane_row == 0, before, turned)
                before = turned
                gas_new[c, i, :, h * LANES : (h + 1) * LANES] = (
                    field[c, h, i] + low
                ) + moved
        pltpu.make_async_copy(
            gas_new.at[:, i], gas_out.at[:, i], plane_sems.at[i]
        ).start()
        return carry

    lax.fori_loop(0, cells_x, finish, 0)

    def settle(i, carry):
        pltpu.make_async_copy(
            gas_new.at[:, i], gas_out.at[:, i], plane_sems.at[i]
        ).wait()
        return carry

    lax.fori_loop(0, cells_x, settle, 0)
    kept.wait()
    fresh.wait()


def neighbour(value, axis, steps):
    count = lax.axis_size(axis)
    pairs = [(source, (source + steps) % count) for source in range(count)]
    return lax.ppermute(value, axis, pairs)


def params(mib):
    return pltpu.CompilerParams(vmem_limit_bytes=mib << 20)


def step(gas_velocity, parcel_z, parcel_velocity, parcel_rate, parcel_mass, parcel_column):
    comps, cells_x, cells_y, depth = gas_velocity.shape
    slots, width = parcel_z.shape
    capacity = slots // 4
    chunks = depth // LANES
    tiles = width // LANES
    cells = cells_x * cells_y
    x_count = lax.axis_size("gx")
    y_count = lax.axis_size(Y_AXES)
    dims = (x_count, y_count, cells_x, cells_y)
    velocity = jnp.transpose(parcel_velocity, (1, 0, 2))
    struct = lambda *shape: jax.ShapeDtypeStruct(shape, F32)

    ext_shape = (comps, chunks, cells_x + 4, cells_y + 2 * SUB, LANES)
    x_up, x_down, y_up, y_down, ext, state = pl.pallas_call(
        faces_kernel,
        out_shape=(
            struct(comps, chunks, 2, cells_y, LANES),
            struct(comps, chunks, 2, cells_y, LANES),
            struct(comps, chunks, 2, cells_x, LANES),
            struct(comps, chunks, 2, cells_x, LANES),
            struct(*ext_shape),
            struct(FIELDS, slots, width),
        ),
        in_specs=[HBM] * 5,
        out_specs=(VMEM,) * 6,
        scratch_shapes=[pltpu.SemaphoreType.DMA((chunks + 4,))],
        compiler_params=params(8),
        name="faces",
    )(gas_velocity, parcel_z, velocity, parcel_rate, parcel_mass)
    x_low = neighbour(x_up, "gx", 1)
    x_high = neighbour(x_down, "gx", -1)
    y_low = neighbour(y_up, Y_AXES, 1)
    y_high = neighbour(y_down, Y_AXES, -1)

    box = struct(FIELDS * capacity + SUB, width)
    outbox = pl.pallas_call(
        functools.partial(pack_kernel, dims, capacity),
        out_shape=(box,) * 4 + (struct(slots, LANES),),
        in_specs=[VMEM] * 2,
        out_specs=(VMEM,) * 5,
        compiler_params=params(8),
        name="pack",
    )(parcel_column.reshape(1, slots), state)
    in0 = neighbour(outbox[0], "gx", 1)
    in1 = neighbour(outbox[1], "gx", -1)

    line = struct(-(-2 * comps * chunks // SUB) * SUB, LANES)
    up, down, box2, box3 = pl.pallas_call(
        relay_kernel,
        out_shape=(line, line, box, box),
        in_specs=[VMEM] * 4,
        out_specs=(VMEM,) * 4,
        input_output_aliases={2: 2, 3: 3},
        compiler_params=params(8),
        name="relay",
    )(x_low, x_high, outbox[2], outbox[3])
    corner_low = neighbour(up, Y_AXES, 1)
    corner_high = neighbour(down, Y_AXES, -1)
    in2 = neighbour(box2, Y_AXES, 1)
    in3 = neighbour(box3, Y_AXES, -1)

    steps = -(-comps * chunks // SUB)
    scratch = [
        pltpu.VMEM((UNROLL, steps, SUB * SUB, LANES), F32),
        pltpu.VMEM((UNROLL, tiles, 2 * SUB * SUB, LANES), F32),
        pltpu.VMEM((UNROLL, tiles, 2 * SUB, LANES), F32),
    ]
    lines, acc, stayed, field, _ = pl.pallas_call(
        functools.partial(stay_kernel, dims),
        out_shape=(
            struct(cells * steps * SUB, LANES),
            struct(cells * chunks * SUB, LANES),
            struct(3, slots, width),
            struct(comps, chunks, cells_x, cells_y, LANES),
            struct(*ext_shape),
        ),
        in_specs=[SMEM] + [VMEM] * 9,
        out_specs=(VMEM,) * 5,
        scratch_shapes=[
            pltpu.VMEM((comps, chunks, cells_x + 2, cells_y + 2 * SUB, LANES), F32),
        ]
        + scratch,
        input_output_aliases={1: 4},
        compiler_params=params(16),
        name="stay",
    )(
        parcel_column,
        ext,
        x_low,
        x_high,
        y_low,
        y_high,
        corner_low,
        corner_high,
        state,
        outbox[4],
    )
    gas_out, updated, _ = pl.pallas_call(
        functools.partial(arrive_kernel, dims, capacity),
        out_shape=(
            struct(comps, cells_x, cells_y, depth),
            struct(3, slots + 4 * capacity, width),
            struct(cells * chunks * SUB, LANES),
        ),
        in_specs=[VMEM] * 8,
        out_specs=(HBM, HBM, VMEM),
        scratch_shapes=[
            pltpu.VMEM((comps, cells_x, cells_y, depth), F32),
            pltpu.VMEM((3, 4 * capacity, width), F32),
        ]
        + scratch
        + [
            pltpu.SMEM((4 * SUB, LANES), F32),
            pltpu.SemaphoreType.DMA((6,)),
            pltpu.SemaphoreType.DMA((cells_x,)),
        ],
        input_output_aliases={5: 2},
        compiler_params=params(16),
        name="arrive",
    )(in0, in1, in2, in3, lines, acc, stayed, field)
    return gas_out, jnp.transpose(updated, (1, 0, 2))


def solution(mesh):
    placed = (
        P(None, "gx", Y_AXES, None),
        P(("grp", "gx", "gy"), None),
        P(("grp", "gx", "gy"), None, None),
        P(("grp", "gx", "gy"), None),
        P(("grp", "gx", "gy"), None),
        P(("grp", "gx", "gy")),
    )
    return jax.shard_map(
        step,
        mesh=mesh,
        in_specs=placed,
        out_specs=(P(None, "gx", Y_AXES, None), P(("grp", "gx", "gy"), None, None)),
        check_vma=False,
    )
```

time: 252 us -> 48.6 us (0.19); the launches traced: 248 us -> 48.3 us
  matrix products: 179 us -> 0 us
  other arithmetic: 23.6 us -> 0 us
  local copies, waits for them, and re-layouts: 24.3 us -> 5.56 us
  Pallas kernels: 0 us -> 15.3 us
  waiting for transfers between devices: 5.32 us -> 11.9 us
    dot_general x26 -> x0, matrix products: 179 us -> none  [the longest x12 98.2 us: couple_group(): jnp.einsum('cbz,bpz->cbp', rows_g, hat, precision=lax.Precision.HIGHEST)]
    pallas_call x0 -> x5, Pallas kernels: none -> 15.3 us  [the longest x1 8.37 us: step(): pl.pallas_call(functools.partial(stay_kernel, dims), out_shape=(struct(ce...]
    mul x12 -> x0, other arithmetic: 9 us -> none  [couple_group(): updated = velocity + relax[None] * (gas_at - velocity)]
    sub x13 -> x0, other arithmetic: 8.72 us -> none  [the longest x12 8.71 us: couple_group(): 1.0 - fraction]
    ppermute x8 -> x10, waiting for transfers between devices: 5.32 us -> 11.9 us  [neighbour(): return lax.ppermute(value, axis, pairs)]
    slice x7 -> x0, local copies, waits for them, and re-layouts: 5.27 us -> none  [the longest x1 1.73 us: with_halo(): lax.slice_in_dim(block, block.shape[dim] - width, None, axis=dim)]
    add x15 -> x0, other arithmetic: 3.58 us -> none  [the longest x2 3.51 us: diffuse_once(): return center + NU * (beside + z_above + z_below - 6.0 * center)]
    unnamed x10 -> x12, local copies, waits for them, and re-layouts: 8.84 us -> 5.56 us
  transfers between devices with their start and end apart: 8 -> 10, of which waited for: 2 -> 3; matrix products, arithmetic and copies ran while one was open for 8% -> 0% of each run, Pallas kernels for 0% -> 18%
where the time goes in v2:
time: 48.6 us; the launch traced here: 48.3 us
  Pallas kernels  15.3 us (31%)
  starting transfers between devices  14.8 us (30%)
  waiting for transfers between devices  11.9 us (24%)
  local copies, waits for them, and re-layouts  5.56 us (11%)
  between operations  0.72 us (1%)
    ppermute x10, starting transfers between devices, neighbour(): return lax.ppermute(value, axis, pairs)  14.8 us
    ppermute x10, waiting for transfers between devices, neighbour(): return lax.ppermute(value, axis, pairs)  11.9 us
    pallas_call x1, Pallas kernels, step(): pl.pallas_call(functools.partial(stay_kernel, dims), out_shape=(struct(ce...  8.37 us
    pallas_call x1, Pallas kernels, step(): pl.pallas_call(functools.partial(arrive_kernel, dims, capacity), out_shap...  5.61 us
    unnamed x12, local copies, waits for them, and re-layouts  5.56 us
  transfers between devices with their start and end apart: 10, of which 3 were waited for; matrix products, arithmetic and copies ran while one was open for 0% of the time, Pallas kernels for 18%

profile of v2, /device:TPU:0, one launch (start us, length us, event | category | flops | bytes accessed | tf_op | source)
XLA Modules:
  0.0 48.3 jit_solution(15907421160418135324)
XLA Ops:
  0.6 0.0 copy-start
  0.6 1.3 %copy-done = f32[3,16,16,384]{3,2,1,0:T(8,128)S(1)} copy-done((f32[3,16,16,384]{3,2,1,0:T(8,128)S(1)}, f32[3,16,16,384]{3,2,1,0:T(8,128)}, u32[]{:S(2)}) %copy-start) | copy-done | bytes 1179672
  1.9 0.0 copy-start.1
  1.9 1.0 %copy-done.1 = f32[96,3,256]{2,0,1:T(8,128)S(1)} copy-done((f32[96,3,256]{2,0,1:T(8,128)S(1)}, f32[96,3,256]{2,0,1:T(8,128)}, u32[]{:S(2)}) %copy-start.1) | copy-done | bytes 294936
  2.9 0.9 %copy-done.2 = f32[96,256]{1,0:T(8,128)S(1)} copy-done((f32[96,256]{1,0:T(8,128)S(1)}, f32[96,256]{1,0:T(8,128)}, u32[]{:S(2)}) %copy-start.2) | copy-done | bytes 98328
  3.8 0.9 %copy-done.3 = f32[96,256]{1,0:T(8,128)S(1)} copy-done((f32[96,256]{1,0:T(8,128)S(1)}, f32[96,256]{1,0:T(8,128)}, u32[]{:S(2)}) %copy-start.3) | copy-done | bytes 98328
  4.7 0.9 %copy-done.4 = f32[96,256]{1,0:T(8,128)S(1)} copy-done((f32[96,256]{1,0:T(8,128)S(1)}, f32[96,256]{1,0:T(8,128)}, u32[]{:S(2)}) %copy-start.4) | copy-done | bytes 98328
  5.5 0.8 %faces.1 = (f32[3,3,2,16,128]{4,3,2,1,0:T(8,128)S(1)}, f32[3,3,2,16,128]{4,3,2,1,0:T(8,128)S(1)}, f32[3,3,2,16,128]{4,3,2,1,0:T(8,128)S(1)}, f32[3,3,2,16,128]{4...) custom-call(f32[3,16,16,384]{3,2,1,0:T(8,128)S(1)} %copy-done, ...), custom_call_target="tpu_custom_call" | custom-call | tf_op jit(solution)/shard_map/faces/pallas_call | solution.py:547
  6.3 3.1 %collective-permute-start.2 = (f32[3,3,2,16,128]{4,3,2,1,0:T(8,128)S(1)}, f32[3,3,2,16,128]{4,3,2,1,0:T(8,128)S(1)}, u32[]{:S(2)}, u32[]{:S(2)}) collective-permute-start(f32[3,3,2,16,128]{4,3,2,1,0:T(8,128)S(1)} %get-tuple-element.26), channel_id=1, source_target_pairs={{0,4},{4,8},{8,12},{12,0},{1,5},{5,9},{9,13},{13,1},{2,6},{6,10},{... | collective-permute-start | bytes 442376 | tf_op jit(solution)/shard_map/ppermute | solution.py:526
  9.4 2.1 %collective-permute-start.3 = (f32[3,3,2,16,128]{4,3,2,1,0:T(8,128)S(1)}, f32[3,3,2,16,128]{4,3,2,1,0:T(8,128)S(1)}, u32[]{:S(2)}, u32[]{:S(2)}) collective-permute-start(f32[3,3,2,16,128]{4,3,2,1,0:T(8,128)S(1)} %get-tuple-element.27), channel_id=1, source_target_pairs={{0,12},{4,0},{8,4},{12,8},{1,13},{5,1},{9,5},{13,9},{2,14},{6,2},{... | collective-permute-start | bytes 442376 | tf_op jit(solution)/shard_map/ppermute | solution.py:526
  11.5 1.6 %collective-permute-start.6 = (f32[3,3,2,16,128]{4,3,2,1,0:T(8,128)S(1)}, f32[3,3,2,16,128]{4,3,2,1,0:T(8,128)S(1)}, u32[]{:S(2)}, u32[]{:S(2)}) collective-permute-start(f32[3,3,2,16,128]{4,3,2,1,0:T(8,128)S(1)} %get-tuple-element.33), channel_id=1, source_target_pairs={{0,1},{1,2},{2,3},{3,16},{16,17},{17,18},{18,19},{19,0},{4,5},{5,6... | collective-permute-start | bytes 442376 | tf_op jit(solution)/shard_map/ppermute | solution.py:526
  13.2 1.0 %collective-permute-start.7 = (f32[3,3,2,16,128]{4,3,2,1,0:T(8,128)S(1)}, f32[3,3,2,16,128]{4,3,2,1,0:T(8,128)S(1)}, u32[]{:S(2)}, u32[]{:S(2)}) collective-permute-start(f32[3,3,2,16,128]{4,3,2,1,0:T(8,128)S(1)} %get-tuple-element.34), channel_id=1, source_target_pairs={{0,19},{1,0},{2,1},{3,2},{16,3},{17,16},{18,17},{19,18},{4,23},{5,... | collective-permute-start | bytes 442376 | tf_op jit(solution)/shard_map/ppermute | solution.py:526
  14.2 0.7 %copy-done.5 = s32[96]{0:T(128)S(1)} copy-done((s32[96]{0:T(128)S(1)}, s32[96]{0:T(128)}, u32[]{:S(2)}) %copy-start.5) | copy-done | bytes 408
  14.8 0.5 %pack.1 = (f32[152,256]{1,0:T(8,128)S(1)}, f32[152,256]{1,0:T(8,128)S(1)}, f32[152,256]{1,0:T(8,128)S(1)}, f32[152,256]{1,0:T(8,128)S(1)}, f32[96,128]{1,0:T(8,128)S(1)}) custom-call(s32[1,96]{1,0:T(1,128)S(1)} %bitcast.4, f32[6,96,256]{2,1,0:T(8,128)S(1)} %get-tuple-element.23.state), custom_call_target="tpu_custom_call" | custom-call | tf_op jit(solution)/shard_map/pack/pallas_call | solution.py:569
  15.4 0.1 collective-permute-start
  15.4 0.8 %collective-permute-done.2.x_low = f32[3,3,2,16,128]{4,3,2,1,0:T(8,128)S(1)} collective-permute-done((f32[3,3,2,16,128]{4,3,2,1,0:T(8,128)S(1)}, f32[3,3,2,16,128]{4,3,2,1,0:T(8,128)S(1)}, u32[]{:S(2)}, u32[]{:S(2)}) %collective-permute-start.2) | collective-permute-done | bytes 147488 | tf_op jit(solution)/shard_map/ppermute | solution.py:526
  16.2 4.1 %collective-permute-start.1 = (f32[152,256]{1,0:T(8,128)S(1)}, f32[152,256]{1,0:T(8,128)S(1)}, u32[]{:S(2)}, u32[]{:S(2)}) collective-permute-start(f32[152,256]{1,0:T(8,128)S(1)} %get-tuple-element.25), channel_id=1, source_target_pairs={{0,12},{4,0},{8,4},{12,8},{1,13},{5,1},{9,5},{13,9},{2,14},{6,2},{... | collective-permute-start | bytes 466952 | tf_op jit(solution)/shard_map/ppermute | solution.py:526
  20.3 0.0 collective-permute-done.3.x_high
  20.4 0.8 %collective-permute-start.4 = (f32[152,256]{1,0:T(8,128)S(1)}, f32[152,256]{1,0:T(8,128)S(1)}, u32[]{:S(2)}, u32[]{:S(2)}) collective-permute-start(f32[152,256]{1,0:T(8,128)S(1)} %get-tuple-element.30), channel_id=1, source_target_pairs={{0,1},{1,2},{2,3},{3,16},{16,17},{17,18},{18,19},{19,0},{4,5},{5,6... | collective-permute-start | bytes 466952 | tf_op jit(solution)/shard_map/ppermute | solution.py:526
  21.1 0.0 collective-permute-done.6.y_low
  21.1 1.9 %collective-permute-start.5 = (f32[152,256]{1,0:T(8,128)S(1)}, f32[152,256]{1,0:T(8,128)S(1)}, u32[]{:S(2)}, u32[]{:S(2)}) collective-permute-start(f32[152,256]{1,0:T(8,128)S(1)} %get-tuple-element.31), channel_id=1, source_target_pairs={{0,19},{1,0},{2,1},{3,2},{16,3},{17,16},{18,17},{19,18},{4,23},{5,... | collective-permute-start | bytes 466952 | tf_op jit(solution)/shard_map/ppermute | solution.py:526
  23.1 0.0 collective-permute-done.7.y_high
  23.1 0.1 collective-permute-start.8
  23.2 7.4 %collective-permute-done.8.corner_low = f32[24,128]{1,0:T(8,128)S(1)} collective-permute-done((f32[24,128]{1,0:T(8,128)S(1)}, f32[24,128]{1,0:T(8,128)S(1)}, u32[]{:S(2)}, u32[]{:S(2)}) %collective-permute-start.8) | collective-permute-done | bytes 12320 | tf_op jit(solution)/shard_map/ppermute | solution.py:526
  30.6 0.0 collective-permute-start.9
  30.6 3.7 %collective-permute-done.9.corner_high = f32[24,128]{1,0:T(8,128)S(1)} collective-permute-done((f32[24,128]{1,0:T(8,128)S(1)}, f32[24,128]{1,0:T(8,128)S(1)}, u32[]{:S(2)}, u32[]{:S(2)}) %collective-permute-start.9) | collective-permute-done | bytes 12320 | tf_op jit(solution)/shard_map/ppermute | solution.py:526
  34.3 8.4 %stay.1 = (f32[4096,128]{1,0:T(8,128)S(1)}, f32[6144,128]{1,0:T(8,128)S(1)}, f32[3,96,256]{2,1,0:T(8,128)S(1)}, f32[3,3,16,16,128]{4,3,2,1,0:T(8,128)S(1)}, f32[3,3,20,32,128]{4,3,2,1,0:T(8,128)S(1)}) custom-call(s32[96]{0:T(128)S(1)} %copy-done.5, f32[3,3,20,32,128]{4,3,2,1,0:T(8,128)S(1)} %get-tuple-element.32.ext_in, ...), custom_call_target="tpu_custom_call", output_to_operand_aliasing={{4}: (1, {})} | custom-call | tf_op jit(solution)/shard_map/stay/pallas_call | solution.py:601
  42.6 0.0 collective-permute-done.in0
  42.6 0.0 collective-permute-done.1.in1
  42.7 0.0 collective-permute-done.4.in2
  42.7 0.0 collective-permute-done.5.in3
  42.7 5.6 %arrive.1 = (f32[3,16,16,384]{3,2,1,0:T(8,128)}, f32[3,192,256]{2,1,0:T(8,128)}, f32[6144,128]{1,0:T(8,128)S(1)}) custom-call(f32[152,256]{1,0:T(8,128)S(1)} %collective-permute-done.in0, f32[152,256]{1,0:T(8,128)S(1)} %collective-permute-done.1.in1, f32[152,256]{1,0:T(8,128)S(1)} %collective-permute-done.4.in2, ...), custom_call_target="tpu_custom_call", output_to_operand_aliasing={{2}: (5, {})} | custom-call | tf_op jit(solution)/shard_map/arrive/pallas_call | solution.py:631
  (5 shorter events, 0.0 us)
Async XLA Ops:
  0.6 1.3 %copy-start = (f32[3,16,16,384]{3,2,1,0:T(8,128)S(1)}, f32[3,16,16,384]{3,2,1,0:T(8,128)}, u32[]{:S(2)}) copy-start(f32[3,16,16,384]{3,2,1,0:T(8,128)} %gas.1) | copy-start | bytes 3538948
  1.9 1.0 %copy-start.1 = (f32[96,3,256]{2,0,1:T(8,128)S(1)}, f32[96,3,256]{2,0,1:T(8,128)}, u32[]{:S(2)}) copy-start(f32[96,3,256]{2,0,1:T(8,128)} %param.8) | copy-start | bytes 884740
  2.9 0.9 %copy-start.2 = (f32[96,256]{1,0:T(8,128)S(1)}, f32[96,256]{1,0:T(8,128)}, u32[]{:S(2)}) copy-start(f32[96,256]{1,0:T(8,128)} %z.1) | copy-start | bytes 294916
  3.8 0.9 %copy-start.3 = (f32[96,256]{1,0:T(8,128)S(1)}, f32[96,256]{1,0:T(8,128)}, u32[]{:S(2)}) copy-start(f32[96,256]{1,0:T(8,128)} %rate.1) | copy-start | bytes 294916
  4.7 0.9 %copy-start.4 = (f32[96,256]{1,0:T(8,128)S(1)}, f32[96,256]{1,0:T(8,128)}, u32[]{:S(2)}) copy-start(f32[96,256]{1,0:T(8,128)} %mass.1) | copy-start | bytes 294916
  6.3 9.9 %collective-permute-start.2 = (f32[3,3,2,16,128]{4,3,2,1,0:T(8,128)S(1)}, f32[3,3,2,16,128]{4,3,2,1,0:T(8,128)S(1)}, u32[]{:S(2)}, u32[]{:S(2)}) collective-permute-start(f32[3,3,2,16,128]{4,3,2,1,0:T(8,128)S(1)} %get-tuple-element.26), channel_id=1, source_target_pairs={{0,4},{4,8},{8,12},{12,0},{1,5},{5,9},{9,13},{13,1},{2,6},{6,10},{... | collective-permute-start | bytes 442376 | tf_op jit(solution)/shard_map/ppermute | solution.py:526
  9.4 10.9 %collective-permute-start.3 = (f32[3,3,2,16,128]{4,3,2,1,0:T(8,128)S(1)}, f32[3,3,2,16,128]{4,3,2,1,0:T(8,128)S(1)}, u32[]{:S(2)}, u32[]{:S(2)}) collective-permute-start(f32[3,3,2,16,128]{4,3,2,1,0:T(8,128)S(1)} %get-tuple-element.27), channel_id=1, source_target_pairs={{0,12},{4,0},{8,4},{12,8},{1,13},{5,1},{9,5},{13,9},{2,14},{6,2},{... | collective-permute-start | bytes 442376 | tf_op jit(solution)/shard_map/ppermute | solution.py:526
  11.5 9.6 %collective-permute-start.6 = (f32[3,3,2,16,128]{4,3,2,1,0:T(8,128)S(1)}, f32[3,3,2,16,128]{4,3,2,1,0:T(8,128)S(1)}, u32[]{:S(2)}, u32[]{:S(2)}) collective-permute-start(f32[3,3,2,16,128]{4,3,2,1,0:T(8,128)S(1)} %get-tuple-element.33), channel_id=1, source_target_pairs={{0,1},{1,2},{2,3},{3,16},{16,17},{17,18},{18,19},{19,0},{4,5},{5,6... | collective-permute-start | bytes 442376 | tf_op jit(solution)/shard_map/ppermute | solution.py:526
  13.2 9.9 %collective-permute-start.7 = (f32[3,3,2,16,128]{4,3,2,1,0:T(8,128)S(1)}, f32[3,3,2,16,128]{4,3,2,1,0:T(8,128)S(1)}, u32[]{:S(2)}, u32[]{:S(2)}) collective-permute-start(f32[3,3,2,16,128]{4,3,2,1,0:T(8,128)S(1)} %get-tuple-element.34), channel_id=1, source_target_pairs={{0,19},{1,0},{2,1},{3,2},{16,3},{17,16},{18,17},{19,18},{4,23},{5,... | collective-permute-start | bytes 442376 | tf_op jit(solution)/shard_map/ppermute | solution.py:526
  14.2 0.7 %copy-start.5 = (s32[96]{0:T(128)S(1)}, s32[96]{0:T(128)}, u32[]{:S(2)}) copy-start(s32[96]{0:T(128)} %columns.1) | copy-start | bytes 1156
  15.4 27.3 %collective-permute-start = (f32[152,256]{1,0:T(8,128)S(1)}, f32[152,256]{1,0:T(8,128)S(1)}, u32[]{:S(2)}, u32[]{:S(2)}) collective-permute-start(f32[152,256]{1,0:T(8,128)S(1)} %get-tuple-element.24), channel_id=1, source_target_pairs={{0,4},{4,8},{8,12},{12,0},{1,5},{5,9},{9,13},{13,1},{2,6},{6,10},{... | collective-permute-start | bytes 466952 | tf_op jit(solution)/shard_map/ppermute | solution.py:526
  16.2 26.4 %collective-permute-start.1 = (f32[152,256]{1,0:T(8,128)S(1)}, f32[152,256]{1,0:T(8,128)S(1)}, u32[]{:S(2)}, u32[]{:S(2)}) collective-permute-start(f32[152,256]{1,0:T(8,128)S(1)} %get-tuple-element.25), channel_id=1, source_target_pairs={{0,12},{4,0},{8,4},{12,8},{1,13},{5,1},{9,5},{13,9},{2,14},{6,2},{... | collective-permute-start | bytes 466952 | tf_op jit(solution)/shard_map/ppermute | solution.py:526
  20.4 22.3 %collective-permute-start.4 = (f32[152,256]{1,0:T(8,128)S(1)}, f32[152,256]{1,0:T(8,128)S(1)}, u32[]{:S(2)}, u32[]{:S(2)}) collective-permute-start(f32[152,256]{1,0:T(8,128)S(1)} %get-tuple-element.30), channel_id=1, source_target_pairs={{0,1},{1,2},{2,3},{3,16},{16,17},{17,18},{18,19},{19,0},{4,5},{5,6... | collective-permute-start | bytes 466952 | tf_op jit(solution)/shard_map/ppermute | solution.py:526
  21.1 21.5 %collective-permute-start.5 = (f32[152,256]{1,0:T(8,128)S(1)}, f32[152,256]{1,0:T(8,128)S(1)}, u32[]{:S(2)}, u32[]{:S(2)}) collective-permute-start(f32[152,256]{1,0:T(8,128)S(1)} %get-tuple-element.31), channel_id=1, source_target_pairs={{0,19},{1,0},{2,1},{3,2},{16,3},{17,16},{18,17},{19,18},{4,23},{5,... | collective-permute-start | bytes 466952 | tf_op jit(solution)/shard_map/ppermute | solution.py:526
  23.1 7.5 %collective-permute-start.8 = (f32[24,128]{1,0:T(8,128)S(1)}, f32[24,128]{1,0:T(8,128)S(1)}, u32[]{:S(2)}, u32[]{:S(2)}) collective-permute-start(f32[24,128]{1,0:T(8,128)S(1)} %get-tuple-element.35), channel_id=1, source_target_pairs={{0,1},{1,2},{2,3},{3,16},{16,17},{17,18},{18,19},{19,0},{4,5},{5,6... | collective-permute-start | bytes 36872 | tf_op jit(solution)/shard_map/ppermute | solution.py:526
  30.6 3.7 %collective-permute-start.9 = (f32[24,128]{1,0:T(8,128)S(1)}, f32[24,128]{1,0:T(8,128)S(1)}, u32[]{:S(2)}, u32[]{:S(2)}) collective-permute-start(f32[24,128]{1,0:T(8,128)S(1)} %get-tuple-element.36), channel_id=1, source_target_pairs={{0,19},{1,0},{2,1},{3,2},{16,3},{17,16},{18,17},{19,18},{4,23},{5,... | collective-permute-start | bytes 36872 | tf_op jit(solution)/shard_map/ppermute | solution.py:526

commit v3 on v2

--- a/solution.py
+++ b/solution.py
@@ -11,7 +11,7 @@
 NU = 0.1
 LANES = 128
 SUB = 8
-UNROLL = 3
+UNROLL = 2
 FIELDS = 6
 Y_AXES = ("grp", "gy")
 F32 = jnp.float32
@@ -63,7 +63,9 @@
     return x * cells_y + remainder(column, cells_y)
 
 
-def faces_kernel(gas, z, v, rate, mass, x_up, x_down, y_up, y_down, ext, state, sems):
+def faces_kernel(
+    gas, z, v, rate, mass, columns, x_up, x_down, y_up, y_down, ext, state, numbers, sems
+):
     comps, cells_x, cells_y, depth = gas.shape
     chunks = depth // LANES
     copies = [
@@ -80,6 +82,7 @@
             (v, state.at[pl.ds(1, 3)]),
             (rate, state.at[4]),
             (mass, state.at[5]),
+            (columns, numbers),
         )
     ):
         copies.append(pltpu.make_async_copy(source, target, sems.at[chunks + i]))
@@ -99,13 +102,47 @@
         copy.wait()
 
 
-def pack_kernel(dims, capacity, columns, state, box0, box1, box2, box3, keep):
+def selected(select, whole):
+    first = whole.astype(BF16)
+    rest = whole - first.astype(F32)
+    second = rest.astype(BF16)
+    third = (rest - second.astype(F32)).astype(BF16)
+    return (
+        jnp.dot(select, first, preferred_element_type=F32)
+        + jnp.dot(select, second, preferred_element_type=F32)
+    ) + jnp.dot(select, third, preferred_element_type=F32)
+
+
+def numbers_at(values, select):
+    slots = values.shape[1]
+    digit = lax.broadcasted_iota(jnp.int32, (SUB, slots), 0)
+    digits = jnp.where(
+        digit == 0,
+        values & 255,
+        jnp.where(digit == 1, (values >> 8) & 255, jnp.where(digit == 2, values >> 16, 0)),
+    )
+    found = lax.dot_general(
+        digits.astype(F32).astype(BF16),
+        select,
+        (((1,), (1,)), ((), ())),
+        preferred_element_type=F32,
+    )
+    return found[0:1] + 256.0 * found[1:2] + 65536.0 * found[2:3]
+
+
+def pack_kernel(dims, capacity, columns, state, box0, box1, box2, box3, keep, late):
     boxes = (box0, box1, box2, box3)
     _, slots, _ = state.shape
+    _, _, cells_x, cells_y = dims
     column = columns[...]
     head = heading_of(column, dims)
+    local = local_of(column, dims)
+    x, y = quotient(local, cells_y), remainder(local, cells_y)
+    waits = (head == 0) & ((x == 0) | (x == cells_x - 1))
+    waits = waits & ((y == 0) | (y == cells_y - 1))
+    head = jnp.where(waits, 5, head)
     code = lax.broadcasted_iota(jnp.int32, (SUB, slots), 0) + 1
-    leaves = jnp.where((code == head) & (code <= 4), 1.0, 0.0)
+    leaves = jnp.where(code == head, 1.0, 0.0)
     before = jnp.where(
         lax.broadcasted_iota(jnp.int32, (slots, slots), 0)
         < lax.broadcasted_iota(jnp.int32, (slots, slots), 1),
@@ -117,39 +154,19 @@
     )
     rank = jnp.sum(ranks * leaves, 0, keepdims=True).astype(jnp.int32)
     target = jnp.where(
-        (head > 0) & (rank < capacity), (head - 1) * capacity + rank, -1
+        (head > 0) & (head < 5) & (rank < capacity), (head - 1) * capacity + rank, -1
     )
     select = jnp.where(
         lax.broadcasted_iota(jnp.int32, (4 * capacity, slots), 0) == target, 1.0, 0.0
     ).astype(BF16)
+    late[...] = jnp.where(head == 5, rank, -1)
     for f in range(FIELDS):
         whole = state[f]
-        first = whole.astype(BF16)
-        rest = whole - first.astype(F32)
-        second = rest.astype(BF16)
-        third = (rest - second.astype(F32)).astype(BF16)
-        moved = (
-            jnp.dot(select, first, preferred_element_type=F32)
-            + jnp.dot(select, second, preferred_element_type=F32)
-        ) + jnp.dot(select, third, preferred_element_type=F32)
+        moved = selected(select, whole)
         for d in range(4):
             boxes[d][f * capacity : (f + 1) * capacity, :] = moved[
                 d * capacity : (d + 1) * capacity
             ]
-    digit = lax.broadcasted_iota(jnp.int32, (SUB, slots), 0)
-    digits = jnp.where(
-        digit == 0,
-        column & 255,
-        jnp.where(
-            digit == 1, (column >> 8) & 255, jnp.where(digit == 2, column >> 16, 0)
-        ),
-    )
-    found = lax.dot_general(
-        digits.astype(F32).astype(BF16),
-        select,
-        (((1,), (1,)), ((), ())),
-        preferred_element_type=F32,
-    )
     same = lax.broadcasted_iota(jnp.int32, (slots, slots), 0)
     same = same == lax.broadcasted_iota(jnp.int32, (slots, slots), 1)
     keep[...] = jnp.dot(
@@ -157,20 +174,55 @@
         jnp.ones((slots, LANES), BF16),
         preferred_element_type=F32,
     )
-    tail = found[0:1] + 256.0 * found[1:2] + 65536.0 * found[2:3]
+    tail = numbers_at(column, select)
     for d in range(4):
         boxes[d][FIELDS * capacity : FIELDS * capacity + 1, 0 : 4 * capacity] = tail
 
 
-def relay_kernel(x_low, x_high, box2, box3, up, down, out2, out3):
-    del box2, box3, out2, out3
-    comps, chunks, _, cells_y, _ = x_low.shape
-    for side, (face, near) in enumerate(((x_low, 1), (x_high, 0))):
+def late_kernel(columns, late, state, box, info, acc):
+    _, slots, _ = state.shape
+    target = late[...]
+    count = jnp.max(target) + 1
+    rank = lax.broadcasted_iota(jnp.int32, (slots, slots), 0)
+    select = jnp.where(rank == target, 1.0, 0.0).astype(BF16)
+    info[0:1, 0:slots] = numbers_at(columns[...], select)
+    slot = lax.broadcasted_iota(jnp.int32, (1, slots), 1)
+    info[1:2, 0:slots] = numbers_at(slot, select)
+    info[2:3, :] = jnp.full((1, info.shape[1]), count, jnp.int32).astype(F32)
+
+    def fill(first, last):
+        for f in range(FIELDS):
+            box[f * slots + first : f * slots + last, :] = selected(
+                select[first:last], state[f]
+            )
+
+    @pl.when(count > 0)
+    def _():
+        fill(0, 2 * SUB)
+
+    @pl.when(count > 2 * SUB)
+    def _():
+        fill(2 * SUB, slots)
+
+    acc[...] = jnp.zeros_like(acc)
+
+
+def line_at(side, c, h, comps, chunks, capacity):
+    line = (side * comps + c) * chunks + h
+    row = FIELDS * capacity + 1 + line // 2
+    lane = line % 2 * LANES
+    return slice(row, row + 1), slice(lane, lane + LANES)
+
+
+def relay_kernel(capacity, y_low, y_high, box0, box1, acc_in, out0, out1, acc):
+    del box0, box1, acc_in, acc
+    comps, chunks, _, cells_x, _ = y_low.shape
+    for side, (face, near) in enumerate(((y_low, 1), (y_high, 0))):
         for c in range(comps):
             for h in range(chunks):
-                row = pl.ds((side * comps + c) * chunks + h, 1)
-                up[row, :] = face[c, h, near, pl.ds(cells_y - 1, 1), :]
-                down[row, :] = face[c, h, near, pl.ds(0, 1), :]
+                rows, lanes = line_at(side, c, h, comps, chunks, capacity)
+                out0[rows, lanes] = face[c, h, near, cells_x - 1 : cells_x, :]
+                out1[rows, lanes] = face[c, h, near, 0:1, :]
 
 
 def stage_one(space, u, zz, vv, rr, mm, local, store):
@@ -268,6 +320,20 @@
             )
 
 
+def pipeline(space, acc, group, count, tiles):
+    waiting = []
+    for start in range(0, count + UNROLL, UNROLL):
+        base = start // UNROLL % 2 * UNROLL
+        fresh = []
+        for u, g in enumerate(range(start, min(start + UNROLL, count))):
+            taken = group(g)
+            stage_one(space, base + u, *taken)
+            fresh.append((base + u, taken[4]))
+        for u, local in waiting:
+            stage_two(space, acc, u, local, tiles)
+        waiting = fresh
+
+
 def mixed(center, x_next, x_last, y_next, y_last):
     chunks = len(center)
     lane = lax.broadcasted_iota(jnp.int32, center[0].shape, 1)
@@ -286,12 +352,13 @@
     dims,
     columns,
     ext_in,
+    acc_in,
     x_low,
     x_high,
     y_low,
     y_high,
-    corner_low,
-    corner_high,
+    y_up,
+    y_down,
     state,
     keep,
     lines,
@@ -304,7 +371,7 @@
     shares,
     marks,
 ):
-    del ext_in
+    del ext_in, acc_in
     _, _, cells_x, cells_y = dims
     comps, chunks = field.shape[:2]
     _, slots, width = state.shape
@@ -312,7 +379,6 @@
     rows = pl.ds(top, cells_y)
     steps = rows_scr.shape[1]
     pitch = steps * SUB
-    acc[...] = jnp.zeros_like(acc)
 
     planes = pl.ds(2, cells_x)
     for c in range(comps):
@@ -321,10 +387,9 @@
             ext[c, h, 2 + cells_x : 4 + cells_x, rows, :] = x_high[c, h]
             ext[c, h, planes, top - 1, :] = y_low[c, h, 1]
             ext[c, h, planes, top + cells_y, :] = y_high[c, h, 0]
-            for corner, y in ((corner_low, top - 1), (corner_high, top + cells_y)):
-                for side, x in ((0, 1), (1, 2 + cells_x)):
-                    line = corner[pl.ds((side * comps + c) * chunks + h, 1), :]
-                    ext[c, h, x, pl.ds(y, 1), :] = line
+            for x in (1, 2 + cells_x):
+                for y in (top - 1, top + cells_y):
+                    ext[c, h, x, y : y + 1, :] = jnp.zeros((1, LANES), F32)
 
     def plane(source, c, x):
         return mixed(
@@ -340,29 +405,25 @@
                 mid[c, h, i, rows, :] = value
         return carry
 
-    lax.fori_loop(0, cells_x + 2, first_plane, 0)
+    lax.fori_loop(0, cells_x + 2, first_plane, 0, unroll=2)
 
     x_row = lax.broadcasted_iota(jnp.int32, (cells_x, LANES), 0)
     for c in range(comps):
-        for face, near, far, inner, corner, row in (
-            (y_low, 1, 0, top, corner_low, top - 1),
-            (y_high, 0, 1, top + cells_y - 1, corner_high, top + cells_y),
+        for side, face, near, far, own, row in (
+            (0, y_low, 1, 0, y_down, top - 1),
+            (1, y_high, 0, 1, y_up, top + cells_y),
         ):
             center = [face[c, h, near] for h in range(chunks)]
             left, right = [], []
             for h in range(chunks):
-                first = corner[pl.ds(c * chunks + h, 1), :]
-                last = corner[pl.ds((comps + c) * chunks + h, 1), :]
-                left.append(jnp.where(x_row == 0, first, pltpu.roll(center[h], 1, 0)))
+                left.append(jnp.where(x_row == 0, 0.0, pltpu.roll(center[h], 1, 0)))
                 right.append(
                     jnp.where(
-                        x_row == cells_x - 1,
-                        last,
-                        pltpu.roll(center[h], cells_x - 1, 0),
+                        x_row == cells_x - 1, 0.0, pltpu.roll(center[h], cells_x - 1, 0)
                     )
                 )
             outer = [face[c, h, far] for h in range(chunks)]
-            inside = [ext[c, h, planes, inner, :] for h in range(chunks)]
+            inside = [own[c, h, side] for h in range(chunks)]
             for h, value in enumerate(mixed(center, left, right, outer, inside)):
                 mid[c, h, pl.ds(1, cells_x), row, :] = value
 
@@ -374,37 +435,26 @@
                 lines[pl.ds(at, cells_y, stride=pitch), :] = value
         return carry
 
-    lax.fori_loop(0, cells_x, second_plane, 0)
+    lax.fori_loop(0, cells_x, second_plane, 0, unroll=2)
+
+    def staying(g):
+        at = pl.ds(g * SUB, SUB)
+        stays = jnp.tile(keep[at, :], (1, width // LANES)) > 0.0
+
+        def store(c, part, value):
+            stayed[c, at, part] = value
+
+        return (
+            state[0, at, :],
+            [jnp.where(stays, state[1 + c, at, :], 0.0) for c in range(3)],
+            jnp.where(stays, state[4, at, :], 0.0),
+            jnp.where(stays, state[5, at, :], 0.0),
+            [local_of(columns[g * SUB + b], dims) for b in range(SUB)],
+            store,
+        )
 
     space = (lines, rows_scr, shares, marks, comps, chunks)
-
-    def staying(g, carry):
-        locals_of = []
-        for u in range(UNROLL):
-            first = pl.multiple_of((g * UNROLL + u) * SUB, SUB)
-            at = pl.ds(first, SUB)
-            stays = jnp.tile(keep[at, :], (1, width // LANES)) > 0.0
-            local = [local_of(columns[first + b], dims) for b in range(SUB)]
-            locals_of.append(local)
-
-            def store(c, part, value, at=at):
-                stayed[c, at, part] = value
-
-            stage_one(
-                space,
-                u,
-                state[0, at, :],
-                [jnp.where(stays, state[1 + c, at, :], 0.0) for c in range(3)],
-                jnp.where(stays, state[4, at, :], 0.0),
-                jnp.where(stays, state[5, at, :], 0.0),
-                local,
-                store,
-            )
-        for u in range(UNROLL):
-            stage_two(space, acc, u, locals_of[u], width // LANES)
-        return carry
-
-    lax.fori_loop(0, slots // SUB // UNROLL, staying, 0)
+    pipeline(space, acc, staying, slots // SUB, width // LANES)
 
 
 def arrive_kernel(
@@ -414,26 +464,33 @@
     in1,
     in2,
     in3,
-    lines,
+    late,
+    info,
+    lines_in,
     acc_in,
-    stayed,
-    field,
+    stayed_in,
+    field_in,
     gas_out,
     parcel_out,
     acc,
+    lines,
+    stayed,
+    field,
     gas_new,
     parcel_new,
     rows_scr,
     shares,
     marks,
     arrived,
+    late_info,
+    one_group,
     sems,
     plane_sems,
 ):
-    del acc_in
+    del lines_in, acc_in, stayed_in, field_in
     _, _, cells_x, cells_y = dims
     comps, chunks = field.shape[:2]
-    _, slots, width = stayed.shape
+    slots, width = stayed.shape[1] - SUB, stayed.shape[2]
     inboxes = (in0, in1, in2, in3)
     tails = [
         pltpu.make_async_copy(
@@ -445,44 +502,77 @@
     ]
     for tail in tails:
         tail.start()
+    listed = pltpu.make_async_copy(info, late_info, sems.at[4])
+    listed.start()
+
+    for inbox, x in ((in0, 0), (in1, cells_x - 1)):
+        for side, y in ((0, 0), (1, cells_y - 1)):
+            for c in range(comps):
+                for h in range(chunks):
+                    rows, lanes = line_at(side, c, h, comps, chunks, capacity)
+                    part = (2.0 * NU * NU) * inbox[rows, lanes]
+                    whole = field[c, h, x, y : y + 1, :] + part
+                    field[c, h, x, y : y + 1, :] = whole
+                    row = (x * cells_y + y) * rows_scr.shape[1] * SUB + c * chunks + h
+                    lines[row : row + 1, :] = whole
+
+    space = (lines, rows_scr, shares, marks, comps, chunks)
+    listed.wait()
+    count = late_info[2, 0].astype(jnp.int32)
+
+    def waited(g, carry):
+        first = pl.multiple_of(g * SUB, SUB)
+        local = [
+            local_of(late_info[0, first + b].astype(jnp.int32), dims)
+            for b in range(SUB)
+        ]
+
+        def store(c, part, value):
+            one_group[c, :, part] = value
+
+        values = [
+            late[pl.ds(pl.multiple_of(first + f * slots, SUB), SUB), :]
+            for f in range(FIELDS)
+        ]
+        stage_one(space, 0, values[0], values[1:4], values[4], values[5], local, store)
+        stage_two(space, acc, 0, local, width // LANES)
+        for b in range(SUB):
+            slot = jnp.where(
+                first + b < count, late_info[1, first + b].astype(jnp.int32), slots
+            )
+            for c in range(3):
+                stayed[c, pl.ds(slot, 1), :] = one_group[c, b : b + 1, :]
+        return carry
+
+    lax.fori_loop(0, (count + SUB - 1) >> 3, waited, 0)
     kept = pltpu.make_async_copy(
-        stayed, parcel_out.at[:, pl.ds(0, slots), :], sems.at[4]
+        stayed.at[:, pl.ds(0, slots), :], parcel_out.at[:, pl.ds(0, slots), :], sems.at[5]
     )
     kept.start()
-    space = (lines, rows_scr, shares, marks, comps, chunks)
     for tail in tails:
         tail.wait()
-    for d in range(4):
-        inbox = inboxes[d]
-        for start in range(0, capacity // SUB, UNROLL):
-            groups = range(start, min(start + UNROLL, capacity // SUB))
-            locals_of = []
-            for u, g in enumerate(groups):
-                first = g * SUB
-                local = [
-                    local_of(
-                        arrived[d * SUB, d * capacity + first + b].astype(jnp.int32),
-                        dims,
-                    )
-                    for b in range(SUB)
-                ]
-                locals_of.append(local)
-                values = [
-                    inbox[first + f * capacity : first + f * capacity + SUB, :]
-                    for f in range(FIELDS)
-                ]
-                row = d * capacity + first
-
-                def store(c, part, value, row=row):
-                    parcel_new[c, row : row + SUB, part] = value
-
-                stage_one(
-                    space, u, values[0], values[1:4], values[4], values[5], local, store
-                )
-            for u, _ in enumerate(groups):
-                stage_two(space, acc, u, locals_of[u], width // LANES)
+    per_box = capacity // SUB
+
+    def arriving(g):
+        d, first = g // per_box, g % per_box * SUB
+        inbox, row = inboxes[d], g * SUB
+        values = [
+            inbox[first + f * capacity : first + f * capacity + SUB, :]
+            for f in range(FIELDS)
+        ]
+
+        def store(c, part, value):
+            parcel_new[c, row : row + SUB, part] = value
+
+        local = [
+            local_of(arrived[d * SUB, row + b].astype(jnp.int32), dims)
+            for b in range(SUB)
+        ]
+        return values[0], values[1:4], values[4], values[5], local, store
+
+    pipeline(space, acc, arriving, 4 * per_box, width // LANES)
     fresh = pltpu.make_async_copy(
-        parcel_new, parcel_out.at[:, pl.ds(slots, 4 * capacity), :], sems.at[5]
+        parcel_new, parcel_out.at[:, pl.ds(slots, 4 * capacity), :], sems.at[6]
     )
     fresh.start()
 
@@ -507,7 +597,7 @@
         ).start()
         return carry
 
-    lax.fori_loop(0, cells_x, finish, 0)
+    lax.fori_loop(0, cells_x, finish, 0, unroll=2)
 
     def settle(i, carry):
         pltpu.make_async_copy(
@@ -544,7 +634,7 @@
     struct = lambda *shape: jax.ShapeDtypeStruct(shape, F32)
 
     ext_shape = (comps, chunks, cells_x + 4, cells_y + 2 * SUB, LANES)
-    x_up, x_down, y_up, y_down, ext, state = pl.pallas_call(
+    x_up, x_down, y_up, y_down, ext, state, numbers = pl.pallas_call(
         faces_kernel,
         out_shape=(
             struct(comps, chunks, 2, cells_y, LANES),
@@ -553,90 +643,126 @@
             struct(comps, chunks, 2, cells_x, LANES),
             struct(*ext_shape),
             struct(FIELDS, slots, width),
+            jax.ShapeDtypeStruct((1, slots), jnp.int32),
         ),
-        in_specs=[HBM] * 5,
-        out_specs=(VMEM,) * 6,
-        scratch_shapes=[pltpu.SemaphoreType.DMA((chunks + 4,))],
+        in_specs=[HBM] * 6,
+        out_specs=(VMEM,) * 7,
+        scratch_shapes=[pltpu.SemaphoreType.DMA((chunks + 5,))],
         compiler_params=params(8),
         name="faces",
-    )(gas_velocity, parcel_z, velocity, parcel_rate, parcel_mass)
+    )(
+        *(
+            pltpu.with_memory_space_constraint(value, pltpu.HBM)
+            for value in (
+                gas_velocity,
+                parcel_z,
+                velocity,
+                parcel_rate,
+                parcel_mass,
+                parcel_column.reshape(1, slots),
+            )
+        )
+    )
     x_low = neighbour(x_up, "gx", 1)
     x_high = neighbour(x_down, "gx", -1)
     y_low = neighbour(y_up, Y_AXES, 1)
     y_high = neighbour(y_down, Y_AXES, -1)
 
     box = struct(FIELDS * capacity + SUB, width)
+    lines_in_box = -(-(1 + comps * chunks) // SUB) * SUB
+    long_box = struct(FIELDS * capacity + lines_in_box, width)
     outbox = pl.pallas_call(
         functools.partial(pack_kernel, dims, capacity),
-        out_shape=(box,) * 4 + (struct(slots, LANES),),
+        out_shape=(
+            long_box,
+            long_box,
+            box,
+            box,
+            struct(slots, LANES),
+            jax.ShapeDtypeStruct((1, slots), jnp.int32),
+        ),
         in_specs=[VMEM] * 2,
-        out_specs=(VMEM,) * 5,
+        out_specs=(VMEM,) * 6,
         compiler_params=params(8),
         name="pack",
-    )(parcel_column.reshape(1, slots), state)
-    in0 = neighbour(outbox[0], "gx", 1)
-    in1 = neighbour(outbox[1], "gx", -1)
-
-    line = struct(-(-2 * comps * chunks // SUB) * SUB, LANES)
-    up, down, box2, box3 = pl.pallas_call(
-        relay_kernel,
-        out_shape=(line, line, box, box),
-        in_specs=[VMEM] * 4,
-        out_specs=(VMEM,) * 4,
-        input_output_aliases={2: 2, 3: 3},
+    )(numbers, state)
+    in2 = neighbour(outbox[2], Y_AXES, 1)
+    in3 = neighbour(outbox[3], Y_AXES, -1)
+
+    acc_struct = struct(cells * chunks * SUB, LANES)
+    late, info, acc = pl.pallas_call(
+        late_kernel,
+        out_shape=(
+            struct(FIELDS * slots, width),
+            struct(SUB, max(LANES, slots)),
+            acc_struct,
+        ),
+        in_specs=[VMEM] * 3,
+        out_specs=(VMEM,) * 3,
+        compiler_params=params(8),
+        name="late",
+    )(numbers, outbox[5], state)
+    box0, box1, acc = pl.pallas_call(
+        functools.partial(relay_kernel, capacity),
+        out_shape=(long_box, long_box, acc_struct),
+        in_specs=[VMEM] * 5,
+        out_specs=(VMEM,) * 3,
+        input_output_aliases={2: 0, 3: 1, 4: 2},
         compiler_params=params(8),
         name="relay",
-    )(x_low, x_high, outbox[2], outbox[3])
-    corner_low = neighbour(up, Y_AXES, 1)
-    corner_high = neighbour(down, Y_AXES, -1)
-    in2 = neighbour(box2, Y_AXES, 1)
-    in3 = neighbour(box3, Y_AXES, -1)
+    )(y_low, y_high, outbox[0], outbox[1], acc)
+    in0 = neighbour(box0, "gx", 1)
+    in1 = neighbour(box1, "gx", -1)
 
     steps = -(-comps * chunks // SUB)
     scratch = [
-        pltpu.VMEM((UNROLL, steps, SUB * SUB, LANES), F32),
-        pltpu.VMEM((UNROLL, tiles, 2 * SUB * SUB, LANES), F32),
-        pltpu.VMEM((UNROLL, tiles, 2 * SUB, LANES), F32),
+        pltpu.VMEM((2 * UNROLL, steps, SUB * SUB, LANES), F32),
+        pltpu.VMEM((2 * UNROLL, tiles, 2 * SUB * SUB, LANES), F32),
+        pltpu.VMEM((2 * UNROLL, tiles, 2 * SUB, LANES), F32),
     ]
     lines, acc, stayed, field, _ = pl.pallas_call(
         functools.partial(stay_kernel, dims),
         out_shape=(
             struct(cells * steps * SUB, LANES),
-            struct(cells * chunks * SUB, LANES),
-            struct(3, slots, width),
+            acc_struct,
+            struct(3, slots + SUB, width),
             struct(comps, chunks, cells_x, cells_y, LANES),
             struct(*ext_shape),
         ),
-        in_specs=[SMEM] + [VMEM] * 9,
+        in_specs=[SMEM] + [VMEM] * 10,
         out_specs=(VMEM,) * 5,
         scratch_shapes=[
             pltpu.VMEM((comps, chunks, cells_x + 2, cells_y + 2 * SUB, LANES), F32),
         ]
         + scratch,
-        input_output_aliases={1: 4},
+        input_output_aliases={1: 4, 2: 1},
         compiler_params=params(16),
         name="stay",
     )(
         parcel_column,
         ext,
+        acc,
         x_low,
         x_high,
         y_low,
         y_high,
-        corner_low,
-        corner_high,
+        y_up,
+        y_down,
         state,
         outbox[4],
     )
-    gas_out, updated, _ = pl.pallas_call(
+    gas_out, updated = pl.pallas_call(
         functools.partial(arrive_kernel, dims, capacity),
         out_shape=(
             struct(comps, cells_x, cells_y, depth),
             struct(3, slots + 4 * capacity, width),
-            struct(cells * chunks * SUB, LANES),
+            acc_struct,
+            struct(cells * steps * SUB, LANES),
+            struct(3, slots + SUB, width),
+            struct(comps, chunks, cells_x, cells_y, LANES),
         ),
-        in_specs=[VMEM] * 8,
-        out_specs=(HBM, HBM, VMEM),
+        in_specs=[VMEM] * 10,
+        out_specs=(HBM, HBM) + (VMEM,) * 4,
         scratch_shapes=[
             pltpu.VMEM((comps, cells_x, cells_y, depth), F32),
             pltpu.VMEM((3, 4 * capacity, width), F32),
@@ -644,13 +770,15 @@
         + scratch
         + [
             pltpu.SMEM((4 * SUB, LANES), F32),
-            pltpu.SemaphoreType.DMA((6,)),
+            pltpu.SMEM((SUB, max(LANES, slots)), F32),
+            pltpu.VMEM((3, SUB, width), F32),
+            pltpu.SemaphoreType.DMA((7,)),
             pltpu.SemaphoreType.DMA((cells_x,)),
         ],
-        input_output_aliases={5: 2},
+        input_output_aliases={6: 3, 7: 2, 8: 4, 9: 5},
         compiler_params=params(16),
         name="arrive",
-    )(in0, in1, in2, in3, lines, acc, stayed, field)
+    )(in0, in1, in2, in3, late, info, lines, acc, stayed, field)[:2]
     return gas_out, jnp.transpose(updated, (1, 0, 2))
 
 

time: 48.6 us -> 37.9 us (0.78)
  local copies, waits for them, and re-layouts: 5.56 us -> 0.01 us
  waiting for transfers between devices: 11.9 us -> 9.3 us
  Pallas kernels: 15.3 us -> 13.7 us
  starting transfers between devices: 14.8 us -> 14.1 us
    unnamed x12 -> x2, local copies, waits for them, and re-layouts: 5.56 us -> 0.01 us
    ppermute x10 -> x8, waiting for transfers between devices: 11.9 us -> 9.3 us  [neighbour(): return lax.ppermute(value, axis, pairs)]
    pallas_call x1, Pallas kernels: 8.37 us -> 6.06 us  [step(): pl.pallas_call(functools.partial(stay_kernel, dims), out_shape=(struct(ce...]
    ppermute x10 -> x8, starting transfers between devices: 14.8 us -> 14.1 us  [neighbour(): return lax.ppermute(value, axis, pairs)]
    pallas_call x1, Pallas kernels: 0.78 us -> 1.5 us  [step(): pl.pallas_call(faces_kernel, out_shape=(struct(comps, chunks, 2, cells_y,...]
  transfers between devices with their start and end apart: 10 -> 8, of which waited for: 3 -> 3; matrix products, arithmetic and copies ran while one was open for 0% -> 0% of each run, Pallas kernels for 18% -> 19%
where the time goes in v3:
time: 37.9 us; the launch traced here: 37.8 us
  starting transfers between devices  14.1 us (37%)
  Pallas kernels  13.7 us (36%)
  waiting for transfers between devices  9.3 us (25%)
  between operations  0.71 us (2%)
    ppermute x8, starting transfers between devices, neighbour(): return lax.ppermute(value, axis, pairs)  14.1 us
    ppermute x8, waiting for transfers between devices, neighbour(): return lax.ppermute(value, axis, pairs)  9.3 us
    pallas_call x1, Pallas kernels, step(): pl.pallas_call(functools.partial(stay_kernel, dims), out_shape=(struct(ce...  6.06 us
    pallas_call x1, Pallas kernels, step(): pl.pallas_call(functools.partial(arrive_kernel, dims, capacity), out_shap...  5.18 us
    pallas_call x1, Pallas kernels, step(): pl.pallas_call(faces_kernel, out_shape=(struct(comps, chunks, 2, cells_y,...  1.5 us
  transfers between devices with their start and end apart: 8, of which 3 were waited for; matrix products, arithmetic and copies ran while one was open for 0% of the time, Pallas kernels for 19%

profile of v3, /device:TPU:0, one launch (start us, length us, event | category | flops | bytes accessed | tf_op | source)
XLA Modules:
  0.0 37.8 jit_solution(17445830644892958976)
XLA Ops:
  0.6 0.0 copy-start
  0.6 1.5 %faces.1 = (f32[3,3,2,16,128]{4,3,2,1,0:T(8,128)S(1)}, f32[3,3,2,16,128]{4,3,2,1,0:T(8,128)S(1)}, f32[3,3,2,16,128]{4,3,2,1,0:T(8,128)S(1)}, f32[3,3,2,16,128]{4...) custom-call(f32[3,16,16,384]{3,2,1,0:T(8,128)} %gas.1, ...), custom_call_target="tpu_custom_call" | custom-call | tf_op jit(solution)/shard_map/faces/pallas_call | solution.py:637
  2.1 3.0 %collective-permute-start = (f32[3,3,2,16,128]{4,3,2,1,0:T(8,128)S(1)}, f32[3,3,2,16,128]{4,3,2,1,0:T(8,128)S(1)}, u32[]{:S(2)}, u32[]{:S(2)}) collective-permute-start(f32[3,3,2,16,128]{4,3,2,1,0:T(8,128)S(1)} %get-tuple-element.27.y_up), channel_id=1, source_target_pairs={{0,1},{1,2},{2,3},{3,16},{16,17},{17,18},{18,19},{19,0},{4,5},{5,6... | collective-permute-start | bytes 442376 | tf_op jit(solution)/shard_map/ppermute | solution.py:616
  5.2 0.5 %collective-permute-start.1 = (f32[3,3,2,16,128]{4,3,2,1,0:T(8,128)S(1)}, f32[3,3,2,16,128]{4,3,2,1,0:T(8,128)S(1)}, u32[]{:S(2)}, u32[]{:S(2)}) collective-permute-start(f32[3,3,2,16,128]{4,3,2,1,0:T(8,128)S(1)} %get-tuple-element.28.y_down), channel_id=1, source_target_pairs={{0,19},{1,0},{2,1},{3,2},{16,3},{17,16},{18,17},{19,18},{4,23},{5,... | collective-permute-start | bytes 442376 | tf_op jit(solution)/shard_map/ppermute | solution.py:616
  5.6 2.3 %collective-permute-start.6 = (f32[3,3,2,16,128]{4,3,2,1,0:T(8,128)S(1)}, f32[3,3,2,16,128]{4,3,2,1,0:T(8,128)S(1)}, u32[]{:S(2)}, u32[]{:S(2)}) collective-permute-start(f32[3,3,2,16,128]{4,3,2,1,0:T(8,128)S(1)} %get-tuple-element.43), channel_id=1, source_target_pairs={{0,4},{4,8},{8,12},{12,0},{1,5},{5,9},{9,13},{13,1},{2,6},{6,10},{... | collective-permute-start | bytes 442376 | tf_op jit(solution)/shard_map/ppermute | solution.py:616
  7.9 0.5 %pack.1 = (f32[160,256]{1,0:T(8,128)S(1)}, f32[160,256]{1,0:T(8,128)S(1)}, f32[152,256]{1,0:T(8,128)S(1)}, f32[152,256]{1,0:T(8,128)S(1)}, f32[96,128]{1,0:T(8,128)S(1)}, /*index=5*/s32[1,96]{1,0:T(1,128)S(1)}) custom-call(s32[1,96]{1,0:T(1,128)S(1)} %get-tuple-element.29.columns, f32[6,96,256]{2,1,0:T(8,128)S(1)} %get-tuple-element.30.state), custom_call_target="tpu_custom_call" | custom-call | tf_op jit(solution)/shard_map/pack/pallas_call | solution.py:674
  8.5 0.4 %late.1 = (f32[576,256]{1,0:T(8,128)S(1)}, f32[8,128]{1,0:T(8,128)S(1)}, f32[6144,128]{1,0:T(8,128)S(1)}) custom-call(s32[1,96]{1,0:T(1,128)S(1)} %get-tuple-element.29.columns, s32[1,96]{1,0:T(1,128)S(1)} %get-tuple-element.33.late, f32[6,96,256]{2,1,0:T(8,128)S(1)} %get-tuple-element.30.state), custom_call_target="tpu_custom_call" | custom-call | tf_op jit(solution)/shard_map/late/pallas_call | solution.py:693
  8.9 0.5 %collective-permute-done.y_low = f32[3,3,2,16,128]{4,3,2,1,0:T(8,128)S(1)} collective-permute-done((f32[3,3,2,16,128]{4,3,2,1,0:T(8,128)S(1)}, f32[3,3,2,16,128]{4,3,2,1,0:T(8,128)S(1)}, u32[]{:S(2)}, u32[]{:S(2)}) %collective-permute-start) | collective-permute-done | bytes 147488 | tf_op jit(solution)/shard_map/ppermute | solution.py:616
  9.4 4.0 %collective-permute-done.1.y_high = f32[3,3,2,16,128]{4,3,2,1,0:T(8,128)S(1)} collective-permute-done((f32[3,3,2,16,128]{4,3,2,1,0:T(8,128)S(1)}, f32[3,3,2,16,128]{4,3,2,1,0:T(8,128)S(1)}, u32[]{:S(2)}, u32[]{:S(2)}) %collective-permute-start.1) | collective-permute-done | bytes 147488 | tf_op jit(solution)/shard_map/ppermute | solution.py:616
  13.4 1.6 %collective-permute-start.2 = (f32[160,256]{1,0:T(8,128)S(1)}, f32[160,256]{1,0:T(8,128)S(1)}, u32[]{:S(2)}, u32[]{:S(2)}) collective-permute-start(f32[160,256]{1,0:T(8,128)S(1)} %get-tuple-element.35), channel_id=1, source_target_pairs={{0,4},{4,8},{8,12},{12,0},{1,5},{5,9},{9,13},{13,1},{2,6},{6,10},{... | collective-permute-start | bytes 491528 | tf_op jit(solution)/shard_map/ppermute | solution.py:616
  15.0 2.2 %collective-permute-start.3 = (f32[160,256]{1,0:T(8,128)S(1)}, f32[160,256]{1,0:T(8,128)S(1)}, u32[]{:S(2)}, u32[]{:S(2)}) collective-permute-start(f32[160,256]{1,0:T(8,128)S(1)} %get-tuple-element.36), channel_id=1, source_target_pairs={{0,12},{4,0},{8,4},{12,8},{1,13},{5,1},{9,5},{13,9},{2,14},{6,2},{... | collective-permute-start | bytes 491528 | tf_op jit(solution)/shard_map/ppermute | solution.py:616
  17.3 1.5 %collective-permute-start.4 = (f32[152,256]{1,0:T(8,128)S(1)}, f32[152,256]{1,0:T(8,128)S(1)}, u32[]{:S(2)}, u32[]{:S(2)}) collective-permute-start(f32[152,256]{1,0:T(8,128)S(1)} %get-tuple-element.37), channel_id=1, source_target_pairs={{0,1},{1,2},{2,3},{3,16},{16,17},{17,18},{18,19},{19,0},{4,5},{5,6... | collective-permute-start | bytes 466952 | tf_op jit(solution)/shard_map/ppermute | solution.py:616
  18.8 1.2 %collective-permute-start.5 = (f32[152,256]{1,0:T(8,128)S(1)}, f32[152,256]{1,0:T(8,128)S(1)}, u32[]{:S(2)}, u32[]{:S(2)}) collective-permute-start(f32[152,256]{1,0:T(8,128)S(1)} %get-tuple-element.38), channel_id=1, source_target_pairs={{0,19},{1,0},{2,1},{3,2},{16,3},{17,16},{18,17},{19,18},{4,23},{5,... | collective-permute-start | bytes 466952 | tf_op jit(solution)/shard_map/ppermute | solution.py:616
  19.9 0.0 collective-permute-done.6.x_low
  19.9 1.8 %collective-permute-start.7 = (f32[3,3,2,16,128]{4,3,2,1,0:T(8,128)S(1)}, f32[3,3,2,16,128]{4,3,2,1,0:T(8,128)S(1)}, u32[]{:S(2)}, u32[]{:S(2)}) collective-permute-start(f32[3,3,2,16,128]{4,3,2,1,0:T(8,128)S(1)} %get-tuple-element.44), channel_id=1, source_target_pairs={{0,12},{4,0},{8,4},{12,8},{1,13},{5,1},{9,5},{13,9},{2,14},{6,2},{... | collective-permute-start | bytes 442376 | tf_op jit(solution)/shard_map/ppermute | solution.py:616
  21.7 4.8 %collective-permute-done.7.x_high = f32[3,3,2,16,128]{4,3,2,1,0:T(8,128)S(1)} collective-permute-done((f32[3,3,2,16,128]{4,3,2,1,0:T(8,128)S(1)}, f32[3,3,2,16,128]{4,3,2,1,0:T(8,128)S(1)}, u32[]{:S(2)}, u32[]{:S(2)}) %collective-permute-start.7) | collective-permute-done | bytes 147488 | tf_op jit(solution)/shard_map/ppermute | solution.py:616
  26.5 0.0 copy-done
  26.5 6.1 %stay.1 = (f32[4096,128]{1,0:T(8,128)S(1)}, f32[6144,128]{1,0:T(8,128)S(1)}, f32[3,104,256]{2,1,0:T(8,128)S(1)}, f32[3,3,16,16,128]{4,3,2,1,0:T(8,128)S(1)}, f32[3,3,20,32,128]{4,3,2,1,0:T(8,128)S(1)}) custom-call(s32[96]{0:T(128)S(1)} %copy-done, f32[3,3,20,32,128]{4,3,2,1,0:T(8,128)S(1)} %get-tuple-element.41.ext_in, ...), custom_call_target="tpu_custom_call", output_to_operand_aliasing={{4}: (1, {}), {1}: (2, {})} | custom-call | tf_op jit(solution)/shard_map/stay/pallas_call | solution.py:723
  32.6 0.0 collective-permute-done.4.in2
  32.6 0.0 collective-permute-done.5.in3
  32.6 0.0 collective-permute-done.2.in0
  32.6 0.0 collective-permute-done.3.in1
  32.6 5.2 %arrive.1 = (f32[3,16,16,384]{3,2,1,0:T(8,128)}, f32[3,192,256]{2,1,0:T(8,128)}, f32[6144,128]{1,0:T(8,128)S(1)}, f32[4096,128]{1,0:T(8,128)S(1)}, f32[3,104,256...) custom-call(f32[160,256]{1,0:T(8,128)S(1)} %collective-permute-done., ...), custom_call_target="tpu_custom_call", output_to_operand_aliasing={{3}: (6, {}), {2}: (7, {}), {4}: (8, {}), {5}: (9, {})} | custom-call | tf_op jit(solution)/shard_map/arrive/pallas_call | solution.py:754
  (1 shorter events, 0.0 us)
Async XLA Ops:
  0.6 25.9 %copy-start = (s32[96]{0:T(128)S(1)}, s32[96]{0:T(128)}, u32[]{:S(2)}) copy-start(s32[96]{0:T(128)} %columns.1) | copy-start | bytes 1156
  2.1 7.3 %collective-permute-start = (f32[3,3,2,16,128]{4,3,2,1,0:T(8,128)S(1)}, f32[3,3,2,16,128]{4,3,2,1,0:T(8,128)S(1)}, u32[]{:S(2)}, u32[]{:S(2)}) collective-permute-start(f32[3,3,2,16,128]{4,3,2,1,0:T(8,128)S(1)} %get-tuple-element.27.y_up), channel_id=1, source_target_pairs={{0,1},{1,2},{2,3},{3,16},{16,17},{17,18},{18,19},{19,0},{4,5},{5,6... | collective-permute-start | bytes 442376 | tf_op jit(solution)/shard_map/ppermute | solution.py:616
  5.2 8.2 %collective-permute-start.1 = (f32[3,3,2,16,128]{4,3,2,1,0:T(8,128)S(1)}, f32[3,3,2,16,128]{4,3,2,1,0:T(8,128)S(1)}, u32[]{:S(2)}, u32[]{:S(2)}) collective-permute-start(f32[3,3,2,16,128]{4,3,2,1,0:T(8,128)S(1)} %get-tuple-element.28.y_down), channel_id=1, source_target_pairs={{0,19},{1,0},{2,1},{3,2},{16,3},{17,16},{18,17},{19,18},{4,23},{5,... | collective-permute-start | bytes 442376 | tf_op jit(solution)/shard_map/ppermute | solution.py:616
  5.6 14.3 %collective-permute-start.6 = (f32[3,3,2,16,128]{4,3,2,1,0:T(8,128)S(1)}, f32[3,3,2,16,128]{4,3,2,1,0:T(8,128)S(1)}, u32[]{:S(2)}, u32[]{:S(2)}) collective-permute-start(f32[3,3,2,16,128]{4,3,2,1,0:T(8,128)S(1)} %get-tuple-element.43), channel_id=1, source_target_pairs={{0,4},{4,8},{8,12},{12,0},{1,5},{5,9},{9,13},{13,1},{2,6},{6,10},{... | collective-permute-start | bytes 442376 | tf_op jit(solution)/shard_map/ppermute | solution.py:616
  13.4 19.2 %collective-permute-start.2 = (f32[160,256]{1,0:T(8,128)S(1)}, f32[160,256]{1,0:T(8,128)S(1)}, u32[]{:S(2)}, u32[]{:S(2)}) collective-permute-start(f32[160,256]{1,0:T(8,128)S(1)} %get-tuple-element.35), channel_id=1, source_target_pairs={{0,4},{4,8},{8,12},{12,0},{1,5},{5,9},{9,13},{13,1},{2,6},{6,10},{... | collective-permute-start | bytes 491528 | tf_op jit(solution)/shard_map/ppermute | solution.py:616
  15.0 17.6 %collective-permute-start.3 = (f32[160,256]{1,0:T(8,128)S(1)}, f32[160,256]{1,0:T(8,128)S(1)}, u32[]{:S(2)}, u32[]{:S(2)}) collective-permute-start(f32[160,256]{1,0:T(8,128)S(1)} %get-tuple-element.36), channel_id=1, source_target_pairs={{0,12},{4,0},{8,4},{12,8},{1,13},{5,1},{9,5},{13,9},{2,14},{6,2},{... | collective-permute-start | bytes 491528 | tf_op jit(solution)/shard_map/ppermute | solution.py:616
  17.3 15.3 %collective-permute-start.4 = (f32[152,256]{1,0:T(8,128)S(1)}, f32[152,256]{1,0:T(8,128)S(1)}, u32[]{:S(2)}, u32[]{:S(2)}) collective-permute-start(f32[152,256]{1,0:T(8,128)S(1)} %get-tuple-element.37), channel_id=1, source_target_pairs={{0,1},{1,2},{2,3},{3,16},{16,17},{17,18},{18,19},{19,0},{4,5},{5,6... | collective-permute-start | bytes 466952 | tf_op jit(solution)/shard_map/ppermute | solution.py:616
  18.8 13.8 %collective-permute-start.5 = (f32[152,256]{1,0:T(8,128)S(1)}, f32[152,256]{1,0:T(8,128)S(1)}, u32[]{:S(2)}, u32[]{:S(2)}) collective-permute-start(f32[152,256]{1,0:T(8,128)S(1)} %get-tuple-element.38), channel_id=1, source_target_pairs={{0,19},{1,0},{2,1},{3,2},{16,3},{17,16},{18,17},{19,18},{4,23},{5,... | collective-permute-start | bytes 466952 | tf_op jit(solution)/shard_map/ppermute | solution.py:616
  19.9 6.6 %collective-permute-start.7 = (f32[3,3,2,16,128]{4,3,2,1,0:T(8,128)S(1)}, f32[3,3,2,16,128]{4,3,2,1,0:T(8,128)S(1)}, u32[]{:S(2)}, u32[]{:S(2)}) collective-permute-start(f32[3,3,2,16,128]{4,3,2,1,0:T(8,128)S(1)} %get-tuple-element.44), channel_id=1, source_target_pairs={{0,12},{4,0},{8,4},{12,8},{1,13},{5,1},{9,5},{13,9},{2,14},{6,2},{... | collective-permute-start | bytes 442376 | tf_op jit(solution)/shard_map/ppermute | solution.py:616

commit v4 on v3

--- a/solution.py
+++ b/solution.py
@@ -11,6 +11,7 @@
 NU = 0.1
 LANES = 128
 SUB = 8
+SPAN = 64
 UNROLL = 2
 FIELDS = 6
 Y_AXES = ("grp", "gy")
@@ -246,8 +247,8 @@
         low_chunk, low_lane = low >> 7, low & (LANES - 1)
         high_chunk, high_lane = high >> 7, high & (LANES - 1)
         relax = rr[:, part] / (1.0 + rr[:, part])
-        marks[u, t, 0:SUB, :] = low_lane.astype(F32)
-        marks[u, t, SUB : 2 * SUB, :] = low_chunk.astype(F32)
+        marks[u, t, 0:SUB, :] = (low & (SPAN - 1)).astype(F32)
+        marks[u, t, SUB : 2 * SUB, :] = (low >> (SPAN.bit_length() - 1)).astype(F32)
         for c in range(comps):
             at_low = at_high = None
             for h in range(chunks):
@@ -278,6 +279,7 @@
 def stage_two(space, acc, u, local, tiles):
     _, _, shares, marks, _, chunks = space
     pack = 2 * SUB
+    per_chunk = LANES // SPAN
     place = lax.broadcasted_iota(jnp.int32, (pack, LANES), 0).astype(F32).astype(BF16)
     one, none = BF16(1.0), BF16(0.0)
     for b in range(SUB):
@@ -285,14 +287,14 @@
         for t in range(tiles):
             share = shares[u, t, pl.ds(b, pack, stride=SUB), :].astype(BF16)
             lane = jnp.broadcast_to(marks[u, t, pl.ds(b, 1), :], (pack, LANES))
-            chunk = jnp.broadcast_to(marks[u, t, pl.ds(SUB + b, 1), :], (pack, LANES))
+            span = jnp.broadcast_to(marks[u, t, pl.ds(SUB + b, 1), :], (pack, LANES))
             offset = lane.astype(BF16) - place
-            chunk = chunk.astype(BF16)
+            span = span.astype(BF16)
             parts.append(
                 jnp.concatenate(
                     [
-                        jnp.where(chunk == BF16(h), share, none)
-                        for h in range(chunks)
+                        jnp.where(span == BF16(q), share, none)
+                        for q in range(chunks * per_chunk)
                     ],
                     0,
                 )
@@ -301,7 +303,7 @@
                 jnp.concatenate(
                     [
                         jnp.where(offset == BF16(pack * i), one, none)
-                        for i in range(LANES // pack)
+                        for i in range(SPAN // pack)
                     ],
                     0,
                 )
@@ -312,11 +314,14 @@
             (((1,), (1,)), ((), ())),
             preferred_element_type=F32,
         )
+        sums = [
+            both[q * pack : q * pack + SUB] + both[q * pack + SUB : (q + 1) * pack]
+            for q in range(chunks * per_chunk)
+        ]
         for h in range(chunks):
             at = pl.ds(pl.multiple_of((local[b] * chunks + h) * SUB, SUB), SUB)
-            row = h * pack
-            acc[at, :] = acc[at, :] + (
-                both[row : row + SUB] + both[row + SUB : row + pack]
+            acc[at, :] = acc[at, :] + jnp.concatenate(
+                sums[h * per_chunk : (h + 1) * per_chunk], 1
             )
 
 
@@ -405,7 +410,7 @@
                 mid[c, h, i, rows, :] = value
         return carry
 
-    lax.fori_loop(0, cells_x + 2, first_plane, 0, unroll=2)
+    lax.fori_loop(0, cells_x + 2, first_plane, 0, unroll=(cells_x + 2) // 2)
 
     x_row = lax.broadcasted_iota(jnp.int32, (cells_x, LANES), 0)
     for c in range(comps):
@@ -435,7 +440,7 @@
                 lines[pl.ds(at, cells_y, stride=pitch), :] = value
         return carry
 
-    lax.fori_loop(0, cells_x, second_plane, 0, unroll=2)
+    lax.fori_loop(0, cells_x, second_plane, 0, unroll=True)
 
     def staying(g):
         at = pl.ds(g * SUB, SUB)
@@ -597,7 +602,7 @@
         ).start()
         return carry
 
-    lax.fori_loop(0, cells_x, finish, 0, unroll=2)
+    lax.fori_loop(0, cells_x, finish, 0, unroll=True)
 
     def settle(i, carry):
         pltpu.make_async_copy(

time: 37.9 us -> 35.2 us (0.929)
  Pallas kernels: 13.7 us -> 10.9 us
    pallas_call x1, Pallas kernels: 6.06 us -> 4.33 us  [step(): pl.pallas_call(functools.partial(stay_kernel, dims), out_shape=(struct(ce...]
    pallas_call x1, Pallas kernels: 5.18 us -> 4.15 us  [step(): pl.pallas_call(functools.partial(arrive_kernel, dims, capacity), out_shap...]
  transfers between devices with their start and end apart: 8 -> 8, of which waited for: 3 -> 3; matrix products, arithmetic and copies ran while one was open for 0% -> 0% of each run, Pallas kernels for 19% -> 15%
where the time goes in v4:
time: 35.2 us; the launch traced here: 35 us
  starting transfers between devices  14.1 us (40%)
  Pallas kernels  10.9 us (31%)
  waiting for transfers between devices  9.3 us (26%)
  between operations  0.7 us (2%)
    ppermute x8, starting transfers between devices, neighbour(): return lax.ppermute(value, axis, pairs)  14.1 us
    ppermute x8, waiting for transfers between devices, neighbour(): return lax.ppermute(value, axis, pairs)  9.3 us
    pallas_call x1, Pallas kernels, step(): pl.pallas_call(functools.partial(stay_kernel, dims), out_shape=(struct(ce...  4.33 us
    pallas_call x1, Pallas kernels, step(): pl.pallas_call(functools.partial(arrive_kernel, dims, capacity), out_shap...  4.15 us
    pallas_call x1, Pallas kernels, step(): pl.pallas_call(faces_kernel, out_shape=(struct(comps, chunks, 2, cells_y,...  1.5 us
  transfers between devices with their start and end apart: 8, of which 3 were waited for; matrix products, arithmetic and copies ran while one was open for 0% of the time, Pallas kernels for 15%

profile of v4, /device:TPU:0, one launch (start us, length us, event | category | flops | bytes accessed | tf_op | source)
XLA Modules:
  0.0 35.0 jit_solution(17085328110794415332)
XLA Ops:
  0.6 0.0 copy-start
  0.6 1.5 %faces.1 = (f32[3,3,2,16,128]{4,3,2,1,0:T(8,128)S(1)}, f32[3,3,2,16,128]{4,3,2,1,0:T(8,128)S(1)}, f32[3,3,2,16,128]{4,3,2,1,0:T(8,128)S(1)}, f32[3,3,2,16,128]{4...) custom-call(f32[3,16,16,384]{3,2,1,0:T(8,128)} %gas.1, ...), custom_call_target="tpu_custom_call" | custom-call | tf_op jit(solution)/shard_map/faces/pallas_call | solution.py:642
  2.1 3.0 %collective-permute-start = (f32[3,3,2,16,128]{4,3,2,1,0:T(8,128)S(1)}, f32[3,3,2,16,128]{4,3,2,1,0:T(8,128)S(1)}, u32[]{:S(2)}, u32[]{:S(2)}) collective-permute-start(f32[3,3,2,16,128]{4,3,2,1,0:T(8,128)S(1)} %get-tuple-element.27.y_up), channel_id=1, source_target_pairs={{0,1},{1,2},{2,3},{3,16},{16,17},{17,18},{18,19},{19,0},{4,5},{5,6... | collective-permute-start | bytes 442376 | tf_op jit(solution)/shard_map/ppermute | solution.py:621
  5.2 0.5 %collective-permute-start.1 = (f32[3,3,2,16,128]{4,3,2,1,0:T(8,128)S(1)}, f32[3,3,2,16,128]{4,3,2,1,0:T(8,128)S(1)}, u32[]{:S(2)}, u32[]{:S(2)}) collective-permute-start(f32[3,3,2,16,128]{4,3,2,1,0:T(8,128)S(1)} %get-tuple-element.28.y_down), channel_id=1, source_target_pairs={{0,19},{1,0},{2,1},{3,2},{16,3},{17,16},{18,17},{19,18},{4,23},{5,... | collective-permute-start | bytes 442376 | tf_op jit(solution)/shard_map/ppermute | solution.py:621
  5.6 2.3 %collective-permute-start.6 = (f32[3,3,2,16,128]{4,3,2,1,0:T(8,128)S(1)}, f32[3,3,2,16,128]{4,3,2,1,0:T(8,128)S(1)}, u32[]{:S(2)}, u32[]{:S(2)}) collective-permute-start(f32[3,3,2,16,128]{4,3,2,1,0:T(8,128)S(1)} %get-tuple-element.43), channel_id=1, source_target_pairs={{0,4},{4,8},{8,12},{12,0},{1,5},{5,9},{9,13},{13,1},{2,6},{6,10},{... | collective-permute-start | bytes 442376 | tf_op jit(solution)/shard_map/ppermute | solution.py:621
  7.9 0.5 %pack.1 = (f32[160,256]{1,0:T(8,128)S(1)}, f32[160,256]{1,0:T(8,128)S(1)}, f32[152,256]{1,0:T(8,128)S(1)}, f32[152,256]{1,0:T(8,128)S(1)}, f32[96,128]{1,0:T(8,128)S(1)}, /*index=5*/s32[1,96]{1,0:T(1,128)S(1)}) custom-call(s32[1,96]{1,0:T(1,128)S(1)} %get-tuple-element.29.columns, f32[6,96,256]{2,1,0:T(8,128)S(1)} %get-tuple-element.30.state), custom_call_target="tpu_custom_call" | custom-call | tf_op jit(solution)/shard_map/pack/pallas_call | solution.py:679
  8.5 0.4 %late.1 = (f32[576,256]{1,0:T(8,128)S(1)}, f32[8,128]{1,0:T(8,128)S(1)}, f32[6144,128]{1,0:T(8,128)S(1)}) custom-call(s32[1,96]{1,0:T(1,128)S(1)} %get-tuple-element.29.columns, s32[1,96]{1,0:T(1,128)S(1)} %get-tuple-element.33.late, f32[6,96,256]{2,1,0:T(8,128)S(1)} %get-tuple-element.30.state), custom_call_target="tpu_custom_call" | custom-call | tf_op jit(solution)/shard_map/late/pallas_call | solution.py:698
  8.9 0.5 %collective-permute-done.y_low = f32[3,3,2,16,128]{4,3,2,1,0:T(8,128)S(1)} collective-permute-done((f32[3,3,2,16,128]{4,3,2,1,0:T(8,128)S(1)}, f32[3,3,2,16,128]{4,3,2,1,0:T(8,128)S(1)}, u32[]{:S(2)}, u32[]{:S(2)}) %collective-permute-start) | collective-permute-done | bytes 147488 | tf_op jit(solution)/shard_map/ppermute | solution.py:621
  9.4 4.0 %collective-permute-done.1.y_high = f32[3,3,2,16,128]{4,3,2,1,0:T(8,128)S(1)} collective-permute-done((f32[3,3,2,16,128]{4,3,2,1,0:T(8,128)S(1)}, f32[3,3,2,16,128]{4,3,2,1,0:T(8,128)S(1)}, u32[]{:S(2)}, u32[]{:S(2)}) %collective-permute-start.1) | collective-permute-done | bytes 147488 | tf_op jit(solution)/shard_map/ppermute | solution.py:621
  13.4 1.6 %collective-permute-start.2 = (f32[160,256]{1,0:T(8,128)S(1)}, f32[160,256]{1,0:T(8,128)S(1)}, u32[]{:S(2)}, u32[]{:S(2)}) collective-permute-start(f32[160,256]{1,0:T(8,128)S(1)} %get-tuple-element.35), channel_id=1, source_target_pairs={{0,4},{4,8},{8,12},{12,0},{1,5},{5,9},{9,13},{13,1},{2,6},{6,10},{... | collective-permute-start | bytes 491528 | tf_op jit(solution)/shard_map/ppermute | solution.py:621
  15.0 2.2 %collective-permute-start.3 = (f32[160,256]{1,0:T(8,128)S(1)}, f32[160,256]{1,0:T(8,128)S(1)}, u32[]{:S(2)}, u32[]{:S(2)}) collective-permute-start(f32[160,256]{1,0:T(8,128)S(1)} %get-tuple-element.36), channel_id=1, source_target_pairs={{0,12},{4,0},{8,4},{12,8},{1,13},{5,1},{9,5},{13,9},{2,14},{6,2},{... | collective-permute-start | bytes 491528 | tf_op jit(solution)/shard_map/ppermute | solution.py:621
  17.3 1.5 %collective-permute-start.4 = (f32[152,256]{1,0:T(8,128)S(1)}, f32[152,256]{1,0:T(8,128)S(1)}, u32[]{:S(2)}, u32[]{:S(2)}) collective-permute-start(f32[152,256]{1,0:T(8,128)S(1)} %get-tuple-element.37), channel_id=1, source_target_pairs={{0,1},{1,2},{2,3},{3,16},{16,17},{17,18},{18,19},{19,0},{4,5},{5,6... | collective-permute-start | bytes 466952 | tf_op jit(solution)/shard_map/ppermute | solution.py:621
  18.8 1.2 %collective-permute-start.5 = (f32[152,256]{1,0:T(8,128)S(1)}, f32[152,256]{1,0:T(8,128)S(1)}, u32[]{:S(2)}, u32[]{:S(2)}) collective-permute-start(f32[152,256]{1,0:T(8,128)S(1)} %get-tuple-element.38), channel_id=1, source_target_pairs={{0,19},{1,0},{2,1},{3,2},{16,3},{17,16},{18,17},{19,18},{4,23},{5,... | collective-permute-start | bytes 466952 | tf_op jit(solution)/shard_map/ppermute | solution.py:621
  19.9 0.0 collective-permute-done.6.x_low
  19.9 1.8 %collective-permute-start.7 = (f32[3,3,2,16,128]{4,3,2,1,0:T(8,128)S(1)}, f32[3,3,2,16,128]{4,3,2,1,0:T(8,128)S(1)}, u32[]{:S(2)}, u32[]{:S(2)}) collective-permute-start(f32[3,3,2,16,128]{4,3,2,1,0:T(8,128)S(1)} %get-tuple-element.44), channel_id=1, source_target_pairs={{0,12},{4,0},{8,4},{12,8},{1,13},{5,1},{9,5},{13,9},{2,14},{6,2},{... | collective-permute-start | bytes 442376 | tf_op jit(solution)/shard_map/ppermute | solution.py:621
  21.7 4.8 %collective-permute-done.7.x_high = f32[3,3,2,16,128]{4,3,2,1,0:T(8,128)S(1)} collective-permute-done((f32[3,3,2,16,128]{4,3,2,1,0:T(8,128)S(1)}, f32[3,3,2,16,128]{4,3,2,1,0:T(8,128)S(1)}, u32[]{:S(2)}, u32[]{:S(2)}) %collective-permute-start.7) | collective-permute-done | bytes 147488 | tf_op jit(solution)/shard_map/ppermute | solution.py:621
  26.5 0.0 copy-done
  26.5 4.3 %stay.1 = (f32[4096,128]{1,0:T(8,128)S(1)}, f32[6144,128]{1,0:T(8,128)S(1)}, f32[3,104,256]{2,1,0:T(8,128)S(1)}, f32[3,3,16,16,128]{4,3,2,1,0:T(8,128)S(1)}, f32[3,3,20,32,128]{4,3,2,1,0:T(8,128)S(1)}) custom-call(s32[96]{0:T(128)S(1)} %copy-done, f32[3,3,20,32,128]{4,3,2,1,0:T(8,128)S(1)} %get-tuple-element.41.ext_in, ...), custom_call_target="tpu_custom_call", output_to_operand_aliasing={{4}: (1, {}), {1}: (2, {})} | custom-call | tf_op jit(solution)/shard_map/stay/pallas_call | solution.py:728
  30.8 0.0 collective-permute-done.4.in2
  30.8 0.0 collective-permute-done.5.in3
  30.9 0.0 collective-permute-done.2.in0
  30.9 0.0 collective-permute-done.3.in1
  30.9 4.1 %arrive.1 = (f32[3,16,16,384]{3,2,1,0:T(8,128)}, f32[3,192,256]{2,1,0:T(8,128)}, f32[6144,128]{1,0:T(8,128)S(1)}, f32[4096,128]{1,0:T(8,128)S(1)}, f32[3,104,256...) custom-call(f32[160,256]{1,0:T(8,128)S(1)} %collective-permute-done., ...), custom_call_target="tpu_custom_call", output_to_operand_aliasing={{3}: (6, {}), {2}: (7, {}), {4}: (8, {}), {5}: (9, {})} | custom-call | tf_op jit(solution)/shard_map/arrive/pallas_call | solution.py:759
  (1 shorter events, 0.0 us)
Async XLA Ops:
  0.6 25.9 %copy-start = (s32[96]{0:T(128)S(1)}, s32[96]{0:T(128)}, u32[]{:S(2)}) copy-start(s32[96]{0:T(128)} %columns.1) | copy-start | bytes 1156
  2.1 7.3 %collective-permute-start = (f32[3,3,2,16,128]{4,3,2,1,0:T(8,128)S(1)}, f32[3,3,2,16,128]{4,3,2,1,0:T(8,128)S(1)}, u32[]{:S(2)}, u32[]{:S(2)}) collective-permute-start(f32[3,3,2,16,128]{4,3,2,1,0:T(8,128)S(1)} %get-tuple-element.27.y_up), channel_id=1, source_target_pairs={{0,1},{1,2},{2,3},{3,16},{16,17},{17,18},{18,19},{19,0},{4,5},{5,6... | collective-permute-start | bytes 442376 | tf_op jit(solution)/shard_map/ppermute | solution.py:621
  5.2 8.2 %collective-permute-start.1 = (f32[3,3,2,16,128]{4,3,2,1,0:T(8,128)S(1)}, f32[3,3,2,16,128]{4,3,2,1,0:T(8,128)S(1)}, u32[]{:S(2)}, u32[]{:S(2)}) collective-permute-start(f32[3,3,2,16,128]{4,3,2,1,0:T(8,128)S(1)} %get-tuple-element.28.y_down), channel_id=1, source_target_pairs={{0,19},{1,0},{2,1},{3,2},{16,3},{17,16},{18,17},{19,18},{4,23},{5,... | collective-permute-start | bytes 442376 | tf_op jit(solution)/shard_map/ppermute | solution.py:621
  5.6 14.3 %collective-permute-start.6 = (f32[3,3,2,16,128]{4,3,2,1,0:T(8,128)S(1)}, f32[3,3,2,16,128]{4,3,2,1,0:T(8,128)S(1)}, u32[]{:S(2)}, u32[]{:S(2)}) collective-permute-start(f32[3,3,2,16,128]{4,3,2,1,0:T(8,128)S(1)} %get-tuple-element.43), channel_id=1, source_target_pairs={{0,4},{4,8},{8,12},{12,0},{1,5},{5,9},{9,13},{13,1},{2,6},{6,10},{... | collective-permute-start | bytes 442376 | tf_op jit(solution)/shard_map/ppermute | solution.py:621
  13.4 17.5 %collective-permute-start.2 = (f32[160,256]{1,0:T(8,128)S(1)}, f32[160,256]{1,0:T(8,128)S(1)}, u32[]{:S(2)}, u32[]{:S(2)}) collective-permute-start(f32[160,256]{1,0:T(8,128)S(1)} %get-tuple-element.35), channel_id=1, source_target_pairs={{0,4},{4,8},{8,12},{12,0},{1,5},{5,9},{9,13},{13,1},{2,6},{6,10},{... | collective-permute-start | bytes 491528 | tf_op jit(solution)/shard_map/ppermute | solution.py:621
  15.0 15.8 %collective-permute-start.3 = (f32[160,256]{1,0:T(8,128)S(1)}, f32[160,256]{1,0:T(8,128)S(1)}, u32[]{:S(2)}, u32[]{:S(2)}) collective-permute-start(f32[160,256]{1,0:T(8,128)S(1)} %get-tuple-element.36), channel_id=1, source_target_pairs={{0,12},{4,0},{8,4},{12,8},{1,13},{5,1},{9,5},{13,9},{2,14},{6,2},{... | collective-permute-start | bytes 491528 | tf_op jit(solution)/shard_map/ppermute | solution.py:621
  17.3 13.6 %collective-permute-start.4 = (f32[152,256]{1,0:T(8,128)S(1)}, f32[152,256]{1,0:T(8,128)S(1)}, u32[]{:S(2)}, u32[]{:S(2)}) collective-permute-start(f32[152,256]{1,0:T(8,128)S(1)} %get-tuple-element.37), channel_id=1, source_target_pairs={{0,1},{1,2},{2,3},{3,16},{16,17},{17,18},{18,19},{19,0},{4,5},{5,6... | collective-permute-start | bytes 466952 | tf_op jit(solution)/shard_map/ppermute | solution.py:621
  18.8 12.1 %collective-permute-start.5 = (f32[152,256]{1,0:T(8,128)S(1)}, f32[152,256]{1,0:T(8,128)S(1)}, u32[]{:S(2)}, u32[]{:S(2)}) collective-permute-start(f32[152,256]{1,0:T(8,128)S(1)} %get-tuple-element.38), channel_id=1, source_target_pairs={{0,19},{1,0},{2,1},{3,2},{16,3},{17,16},{18,17},{19,18},{4,23},{5,... | collective-permute-start | bytes 466952 | tf_op jit(solution)/shard_map/ppermute | solution.py:621
  19.9 6.6 %collective-permute-start.7 = (f32[3,3,2,16,128]{4,3,2,1,0:T(8,128)S(1)}, f32[3,3,2,16,128]{4,3,2,1,0:T(8,128)S(1)}, u32[]{:S(2)}, u32[]{:S(2)}) collective-permute-start(f32[3,3,2,16,128]{4,3,2,1,0:T(8,128)S(1)} %get-tuple-element.44), channel_id=1, source_target_pairs={{0,12},{4,0},{8,4},{12,8},{1,13},{5,1},{9,5},{13,9},{2,14},{6,2},{... | collective-permute-start | bytes 442376 | tf_op jit(solution)/shard_map/ppermute | solution.py:621
